TPU v7x, 512 devices: a whole 4x8x8 slice. The times are simulated.
512 devices in a mesh: row: 16 (over z, core), col: 32 (over x, y).
Axes of the slice: x: 4, y: 8, z: 8, core: 2. Of those that a mesh axis runs over, the one named last changes fastest.
Arguments:
- graph_emb: float32 [16384, 256], P('row', 'col'), may hold values from -40 to 40
- conf_emb: float32 [16384, 256], P('col', 'row'), may hold values from -40 to 40
Outputs:
- grad_graph: float32 [16384, 256], P('row', 'col')
- grad_conf: float32 [16384, 256], P('col', 'row')
- row_potential: float32 [16384], P('row')
- col_potential: float32 [16384], P('col')
All inputs are finite; a program needn't handle non-finite values.
Results may differ from a plain program's by a relative error of at most 0.0003.
Values sent between devices are 32-bit elements; how exact they have to be, the bound alone decides.
No kernel may reach another device: no remote copies, remote signals or barrier semaphores. Data moves between devices by JAX's collectives and lax.ppermute only.
A program may use at most 64 MiB of HBM per device.

v0:
```python
import math

import jax
import jax.numpy as jnp
from jax import lax
from jax.sharding import PartitionSpec as P

ITERS = 3


entropy_weight = 1.0


def across_columns(scores):
    local_max = jnp.max(scores, axis=1)
    peak_value = lax.pmax(local_max, "col")
    exp_total = lax.psum(jnp.sum(jnp.exp(scores - peak_value[:, None]), axis=1), "col")
    return peak_value + jnp.log(exp_total)


def across_rows(scores):
    local_max = jnp.max(scores, axis=0)
    peak_value = lax.pmax(local_max, "row")
    exp_total = lax.psum(jnp.sum(jnp.exp(scores - peak_value[None, :]), axis=0), "row")
    return peak_value + jnp.log(exp_total)


def per_device(graph_emb, conf_emb):
    graph_block = lax.all_gather(graph_emb, "col", axis=1, tiled=True)
    conf_block = lax.all_gather(conf_emb, "row", axis=1, tiled=True)
    batch_size = graph_block.shape[0] * lax.axis_size("row")
    feature_scale = graph_block.shape[1] ** (-0.5)
    cost_tile = (
        -lax.dot_general(
            graph_block,
            conf_block,
            (((1,), (1,)), ((), ())),
            precision=lax.Precision.HIGHEST,
            preferred_element_type=jnp.float32,
        )
        * feature_scale
    )
    log_weight = -math.log(batch_size)
    row_pot = jnp.zeros((graph_block.shape[0],), jnp.float32)
    col_pot = jnp.zeros((conf_block.shape[0],), jnp.float32)
    for sweep_index in range(ITERS):
        row_pot = entropy_weight * (
            log_weight - across_columns((col_pot[None, :] - cost_tile) / entropy_weight)
        )
        col_pot = entropy_weight * (
            log_weight - across_rows((row_pot[:, None] - cost_tile) / entropy_weight)
        )
    transport = jnp.exp((row_pot[:, None] + col_pot[None, :] - cost_tile) / entropy_weight)
    factor = -batch_size * feature_scale
    graph_term = (
        jnp.dot(
            transport,
            conf_block,
            precision=lax.Precision.HIGHEST,
            preferred_element_type=jnp.float32,
        )
        * factor
    )
    conf_term = (
        lax.dot_general(
            transport,
            graph_block,
            (((0,), (0,)), ((), ())),
            precision=lax.Precision.HIGHEST,
            preferred_element_type=jnp.float32,
        )
        * factor
    )
    graph_total = lax.psum(graph_term, "col")
    conf_total = lax.psum(conf_term, "row")
    graph_width = graph_term.shape[1] // lax.axis_size("col")
    conf_width = conf_term.shape[1] // lax.axis_size("row")
    grad_graph = lax.dynamic_slice_in_dim(
        graph_total, lax.axis_index("col") * graph_width, graph_width, 1
    )
    grad_conf = lax.dynamic_slice_in_dim(
        conf_total, lax.axis_index("row") * conf_width, conf_width, 1
    )
    return (grad_graph, grad_conf, row_pot, col_pot)


def solution(mesh):
    return jax.shard_map(
        per_device,
        mesh=mesh,
        in_specs=(P("row", "col"), P("col", "row")),
        out_specs=(P("row", "col"), P("col", "row"), P("row"), P("col")),
        check_vma=False,
    )
```

profile of v0, /device:TPU:1, one launch (start us, length us, event | category | flops | bytes accessed | tf_op | source)
XLA Modules:
  0.0 955.8 jit_solution(13728568763963591692)
XLA Ops:
  7.2 0.7 all-gather.2.cloned.1.call-update
  7.9 26.2 %all_gather.7 = f32[512,256]{0,1:T(8,128)S(1)} all-gather(f32[512,16]{0,1:T(8,128)} %param.3), channel_id=1, replica_groups=mesh['row'=16,'col'=32] {'row'}, dimensions={1}, use_global_device_ids=true | all-gather | bytes 557056 | tf_op jit(solution)/shard_map/all_gather | solution.py:30
  34.1 59.2 %all-gather.2.cloned.1.call-done = f32[1024,256]{0,1:T(8,128)} async-done(((f32[1024,8]{0,1:T(8,128)}), f32[1024,256]{0,1:T(8,128)}) %all-gather.2.cloned.1.call-update) | async-done | bytes 1048592 | tf_op jit(solution)/shard_map/all_gather | solution.py:29
  93.3 3.2 subtract_reduce_fusion.5
  96.6 57.9 %pmax.42 = f32[1024]{0:T(1024)S(1)} all-reduce(f32[1024]{0:T(1024)S(1)} %get-tuple-element.4), channel_id=1, replica_groups=mesh['row'=16,'col'=32] {'col'}, use_global_device_ids=true, to_apply=%region_1.0 | all-reduce | flops 1024 | bytes 8192 | tf_op jit(solution)/shard_map/pmax | solution.py:16
  154.5 0.5 exponential_reduce_fusion.5
  155.0 55.8 %psum.56 = f32[1024]{0:T(1024)S(1)} all-reduce(f32[1024]{0:T(1024)S(1)} %exponential_reduce_fusion.5), channel_id=1, replica_groups=mesh['row'=16,'col'=32] {'col'}, use_global_device_ids=true, to_apply=%region_3.0 | all-reduce | flops 1024 | bytes 8192 | tf_op jit(solution)/shard_map/psum | solution.py:17
  210.9 0.2 subtract_reduce_fusion.4
  211.1 57.5 %pmax.43 = f32[512]{0:T(512)S(1)} all-reduce(f32[512]{0:T(512)S(1)} %subtract_reduce_fusion.4), channel_id=1, replica_groups=mesh['row'=16,'col'=32] {'row'}, use_global_device_ids=true, to_apply=%region_5.0 | all-reduce | flops 512 | bytes 4096 | tf_op jit(solution)/shard_map/pmax | solution.py:23
  268.6 0.4 exponential_reduce_fusion.4
  269.1 23.1 %psum.57 = f32[512]{0:T(512)S(1)} all-reduce(f32[512]{0:T(512)S(1)} %exponential_reduce_fusion.4), channel_id=1, replica_groups=mesh['row'=16,'col'=32] {'row'}, use_global_device_ids=true, to_apply=%region_7.0 | all-reduce | flops 512 | bytes 4096 | tf_op jit(solution)/shard_map/psum | solution.py:24
  292.4 57.7 %pmax.44 = f32[1024]{0:T(1024)S(1)} all-reduce(f32[1024]{0:T(1024)S(1)} %subtract_reduce_fusion.3), channel_id=1, replica_groups=mesh['row'=16,'col'=32] {'col'}, use_global_device_ids=true, to_apply=%region_9.0 | all-reduce | flops 1024 | bytes 8192 | tf_op jit(solution)/shard_map/pmax | solution.py:16
  350.0 0.6 exponential_reduce_fusion.3
  350.6 56.2 %psum.58 = f32[1024]{0:T(1024)S(1)} all-reduce(f32[1024]{0:T(1024)S(1)} %exponential_reduce_fusion.3), channel_id=1, replica_groups=mesh['row'=16,'col'=32] {'col'}, use_global_device_ids=true, to_apply=%region_11.0 | all-reduce | flops 1024 | bytes 8192 | tf_op jit(solution)/shard_map/psum | solution.py:17
  406.8 0.2 subtract_reduce_fusion.2
  407.1 51.3 %pmax.45 = f32[512]{0:T(512)S(1)} all-reduce(f32[512]{0:T(512)S(1)} %subtract_reduce_fusion.2), channel_id=1, replica_groups=mesh['row'=16,'col'=32] {'row'}, use_global_device_ids=true, to_apply=%region_13.0 | all-reduce | flops 512 | bytes 4096 | tf_op jit(solution)/shard_map/pmax | solution.py:23
  458.4 0.4 exponential_reduce_fusion.2
  458.8 23.5 %psum.59 = f32[512]{0:T(512)S(1)} all-reduce(f32[512]{0:T(512)S(1)} %exponential_reduce_fusion.2), channel_id=1, replica_groups=mesh['row'=16,'col'=32] {'row'}, use_global_device_ids=true, to_apply=%region_15.0 | all-reduce | flops 512 | bytes 4096 | tf_op jit(solution)/shard_map/psum | solution.py:24
  482.6 57.4 %pmax.46 = f32[1024]{0:T(1024)S(1)} all-reduce(f32[1024]{0:T(1024)S(1)} %subtract_reduce_fusion.1), channel_id=1, replica_groups=mesh['row'=16,'col'=32] {'col'}, use_global_device_ids=true, to_apply=%region_17.0 | all-reduce | flops 1024 | bytes 8192 | tf_op jit(solution)/shard_map/pmax | solution.py:16
  540.0 0.6 exponential_reduce_fusion.1
  540.6 56.1 %psum.60 = f32[1024]{0:T(1024)S(1)} all-reduce(f32[1024]{0:T(1024)S(1)} %exponential_reduce_fusion.1), channel_id=1, replica_groups=mesh['row'=16,'col'=32] {'col'}, use_global_device_ids=true, to_apply=%region_19.0 | all-reduce | flops 1024 | bytes 8192 | tf_op jit(solution)/shard_map/psum | solution.py:17
  596.7 0.2 subtract_reduce_fusion
  596.9 51.3 %pmax.47 = f32[512]{0:T(512)S(1)} all-reduce(f32[512]{0:T(512)S(1)} %subtract_reduce_fusion), channel_id=1, replica_groups=mesh['row'=16,'col'=32] {'row'}, use_global_device_ids=true, to_apply=%region_21.0 | all-reduce | flops 512 | bytes 4096 | tf_op jit(solution)/shard_map/pmax | solution.py:23
  648.2 0.4 exponential_reduce_fusion
  648.6 23.5 %psum.61 = f32[512]{0:T(512)S(1)} all-reduce(f32[512]{0:T(512)S(1)} %exponential_reduce_fusion), channel_id=1, replica_groups=mesh['row'=16,'col'=32] {'row'}, use_global_device_ids=true, to_apply=%region_23.0 | all-reduce | flops 512 | bytes 4096 | tf_op jit(solution)/shard_map/psum | solution.py:24
  672.2 4.4 fusion.3
  676.6 0.2 all-reduce.3.cloned.1.call-start
  676.9 3.4 fusion.2
  680.3 107.9 %all-reduce.5.cloned.1.call-done = f32[512,256]{0,1:T(8,128)} async-done(((f32[512,256]{0,1:T(8,128)}), f32[512,256]{0,1:T(8,128)}) %all-reduce.5.cloned.1.call-update) | async-done | bytes 524304 | tf_op jit(solution)/shard_map/psum | solution.py:75
  788.2 1.4 constant_dynamic-slice_fusion
  789.6 158.4 %all-reduce.3.cloned.1.call-done = f32[1024,256]{0,1:T(8,128)} async-done(((f32[1024,256]{0,1:T(8,128)}), f32[1024,256]{0,1:T(8,128)}) %all-reduce.3.cloned.1.call-update) | async-done | bytes 1048592 | tf_op jit(solution)/shard_map/psum | solution.py:74
  947.9 1.4 constant_dynamic-slice_fusion.1
  (16 shorter events, 0.6 us)
Async XLA Ops:
  7.2 86.2 %all-gather.2.cloned.1.call-start = ((), (), s32[]{:S(2)}) async-start(), calls=%async_computation | async-start | bytes 1081344 | tf_op jit(solution)/shard_map/all_gather | solution.py:29
  7.9 780.3 %all-reduce.5.cloned.1.call-start = ((), (), s32[]{:S(2)}) async-start(), calls=%async_computation.2 | async-start | bytes 1048576 | tf_op jit(solution)/shard_map/psum | solution.py:75
  596.7 80.2 %copy-start = (f32[1024]{0:T(1024)}, f32[1024]{0:T(1024)S(1)}, u32[]{:S(2)}) copy-start(f32[1024]{0:T(1024)S(1)} %add_subtract_fusion) | copy-start | bytes 12292
  672.2 4.7 copy-start.1
  676.6 271.3 %all-reduce.3.cloned.1.call-start = ((), (), s32[]{:S(2)}) async-start(), calls=%async_computation.1 | async-start | bytes 2097152 | tf_op jit(solution)/shard_map/psum | solution.py:74
Sparse Core Ops, SparseCore 0:
  11.1 82.1 all-gather.1
  676.7 111.4 all-reduce.4
  791.6 156.2 all-reduce.2
where the time goes:
time: 960 us; the launch traced here: 956 us
  blocking collectives  598 us (62%)
  waiting for transfers between devices  326 us (34%)
  between operations  13.8 us (1%)
  matrix products  11 us (1%)
    pmax x3, blocking collectives, across_columns(): peak_value = lax.pmax(local_max, 'col')  173 us
    psum x3, blocking collectives, across_columns(): lax.psum(jnp.sum(jnp.exp(scores - peak_value[:, None]), axis=1), 'col')  168 us
    pmax x3, blocking collectives, across_rows(): peak_value = lax.pmax(local_max, 'row')  160 us
    psum x1, waiting for transfers between devices, per_device(): graph_total = lax.psum(graph_term, 'col')  158 us
    psum x1, waiting for transfers between devices, per_device(): conf_total = lax.psum(conf_term, 'row')  108 us
    psum x3, blocking collectives, across_rows(): lax.psum(jnp.sum(jnp.exp(scores - peak_value[None, :]), axis=0), 'row')  70.2 us
    all_gather x1, waiting for transfers between devices, per_device(): graph_block = lax.all_gather(graph_emb, 'col', axis=1, tiled=True)  59.2 us
    all_gather x1, blocking collectives, per_device(): conf_block = lax.all_gather(conf_emb, 'row', axis=1, tiled=True)  26.2 us
  transfers between devices with their start and end apart: 3, of which 3 were waited for; matrix products, arithmetic and copies ran while one was open for 0% of the time, Pallas kernels for 0%

commit v1 on v0

v1 whole, which is shorter than its diff:
```python
import math

import jax
import jax.numpy as jnp
from jax import lax
from jax.sharding import PartitionSpec as P

ITERS = 3
LANES = 128


def spread(block, axis):
    n = lax.axis_size(axis)
    return lax.all_to_all(jnp.broadcast_to(block[None], (n,) + block.shape), axis, 0, 0)


def swap(chunks, axis):
    return lax.all_to_all(chunks, axis, 0, 0)


def lse(values, dim):
    peak = jnp.max(values, axis=dim, keepdims=True)
    total = jnp.sum(jnp.exp(values - peak), axis=dim)
    return jnp.squeeze(peak, dim) + jnp.log(total)


def shared_lse(partial, axis):
    parts = spread(partial.reshape(-1, LANES), axis)
    return lse(parts, 0).reshape(partial.shape)


def per_device(graph_emb, conf_emb):
    graph_part, conf_part = graph_emb.T, conf_emb.T
    conf_t = spread(conf_part, "row").reshape(-1, conf_part.shape[1])
    graph_t = spread(graph_part, "col").reshape(-1, graph_part.shape[1])
    width, rows = graph_t.shape
    cols = conf_t.shape[1]
    batch = rows * lax.axis_size("row")
    scale = width ** (-0.5)
    score = (
        lax.dot_general(
            graph_t,
            conf_t,
            (((0,), (0,)), ((), ())),
            precision=lax.Precision.HIGHEST,
            preferred_element_type=jnp.float32,
        )
        * scale
    )
    log_weight = -math.log(batch)
    row_pot = jnp.zeros((rows,), jnp.float32)
    col_pot = jnp.zeros((cols,), jnp.float32)
    for _ in range(ITERS):
        row_pot = log_weight - shared_lse(lse(col_pot[None, :] + score, 1), "col")
        col_pot = log_weight - shared_lse(lse(row_pot[:, None] + score, 0), "row")
    plan = jnp.exp(row_pot[:, None] + col_pot[None, :] + score)
    factor = -batch * scale
    conf_term = (
        lax.dot_general(
            graph_t,
            plan,
            (((1,), (0,)), ((), ())),
            precision=lax.Precision.HIGHEST,
            preferred_element_type=jnp.float32,
        )
        * factor
    )
    graph_term = (
        lax.dot_general(
            conf_t,
            plan,
            (((1,), (1,)), ((), ())),
            precision=lax.Precision.HIGHEST,
            preferred_element_type=jnp.float32,
        )
        * factor
    )
    conf_parts = swap(conf_term.reshape(lax.axis_size("row"), -1, cols), "row")
    graph_parts = swap(graph_term.reshape(lax.axis_size("col"), -1, rows), "col")
    grad_conf = jnp.sum(conf_parts, axis=0).T
    grad_graph = jnp.sum(graph_parts, axis=0).T
    return (grad_graph, grad_conf, row_pot, col_pot)


def solution(mesh):
    return jax.shard_map(
        per_device,
        mesh=mesh,
        in_specs=(P("row", "col"), P("col", "row")),
        out_specs=(P("row", "col"), P("col", "row"), P("row"), P("col")),
        check_vma=False,
    )
```

time: 960 us -> 211 us (0.22)
  blocking collectives: 598 us -> 142 us
  waiting for transfers between devices: 326 us -> 41.4 us
  between operations: 13.8 us -> 0.82 us
    pmax x6 -> x0, blocking collectives: 333 us -> none  [the longest x3 173 us: across_columns(): peak_value = lax.pmax(local_max, 'col')]
    psum x2 -> x0, waiting for transfers between devices: 266 us -> none  [the longest x1 158 us: per_device(): graph_total = lax.psum(graph_term, 'col')]
    psum x6 -> x0, blocking collectives: 238 us -> none  [the longest x3 168 us: across_columns(): lax.psum(jnp.sum(jnp.exp(scores - peak_value[:, None]), axis=1), 'col')]
    all_to_all x0 -> x8, blocking collectives: none -> 142 us  [spread(): lax.all_to_all(jnp.broadcast_to(block[None], (n,) + block.shape), axis, 0...]
    all_gather x1 -> x0, waiting for transfers between devices: 59.2 us -> none  [per_device(): graph_block = lax.all_gather(graph_emb, 'col', axis=1, tiled=True)]
    all_to_all x0 -> x2, waiting for transfers between devices: none -> 41.4 us  [swap(): return lax.all_to_all(chunks, axis, 0, 0)]
    all_gather x1 -> x0, blocking collectives: 26.2 us -> none  [per_device(): conf_block = lax.all_gather(conf_emb, 'row', axis=1, tiled=True)]
  transfers between devices with their start and end apart: 3 -> 2, of which waited for: 3 -> 2; matrix products, arithmetic and copies ran while one was open for 0% -> 2% of each run, Pallas kernels for 0% -> 0%
where the time goes in v1:
time: 211 us; the launch traced here: 210 us
  blocking collectives  142 us (67%)
  waiting for transfers between devices  41.4 us (20%)
  matrix products  9.69 us (5%)
  starting transfers between devices  7.68 us (4%)
  other arithmetic  6.09 us (3%)
  local copies, waits for them, and re-layouts  2.72 us (1%)
    all_to_all x8, blocking collectives, spread(): lax.all_to_all(jnp.broadcast_to(block[None], (n,) + block.shape), axis, 0...  142 us
    all_to_all x2, waiting for transfers between devices, swap(): return lax.all_to_all(chunks, axis, 0, 0)  41.4 us
    all_to_all x2, starting transfers between devices, swap(): return lax.all_to_all(chunks, axis, 0, 0)  7.68 us
    dot_general x1, matrix products, per_device(): lax.dot_general(graph_t, plan, (((1,), (0,)), ((), ())), precision=lax.Pr...  4.43 us
  transfers between devices with their start and end apart: 2, of which 2 were waited for; matrix products, arithmetic and copies ran while one was open for 2% of the time, Pallas kernels for 0%

profile of v1, /device:TPU:1, one launch (start us, length us, event | category | flops | bytes accessed | tf_op | source)
XLA Modules:
  0.0 210.0 jit_solution(8133503578238404256)
XLA Ops:
  0.6 0.8 broadcast_in_dim.17
  1.4 28.8 %all_to_all.50 = f32[16,16,512]{2,1,0:T(8,128)S(1)} all-to-all(f32[16,16,512]{2,1,0:T(8,128)S(1)} %broadcast_in_dim.17), channel_id=1, replica_groups=mesh['row'=16,'col'=32] {'row'}, dimensions={0} | all-to-all | bytes 1048576 | tf_op jit(solution)/shard_map/all_to_all | solution.py:14
  30.3 0.9 broadcast_in_dim.16
  31.1 37.7 %all_to_all.51 = f32[32,8,1024]{2,1,0:T(8,128)S(1)} all-to-all(f32[32,8,1024]{2,1,0:T(8,128)S(1)} %broadcast_in_dim.16), channel_id=1, replica_groups=mesh['row'=16,'col'=32] {'col'}, dimensions={0} | all-to-all | bytes 2097152 | tf_op jit(solution)/shard_map/all_to_all | solution.py:14
  68.8 1.0 copy-done
  69.8 1.9 fusion.11
  71.7 0.7 exponential_reduce_fusion.5
  72.5 14.2 %all_to_all.52 = f32[32,8,128]{2,1,0:T(8,128)S(1)} all-to-all(f32[32,8,128]{2,1,0:T(8,128)S(1)} %broadcast_in_dim.18), channel_id=1, replica_groups=mesh['row'=16,'col'=32] {'col'}, dimensions={0} | all-to-all | bytes 262144 | tf_op jit(solution)/shard_map/all_to_all | solution.py:14
  86.8 0.2 add_reduce_fusion.4
  87.0 0.4 exponential_reduce_fusion.4
  87.5 12.3 %all_to_all.53 = f32[16,4,128]{2,1,0:T(4,128)S(1)} all-to-all(f32[16,4,128]{2,1,0:T(4,128)S(1)} %broadcast_in_dim.19), channel_id=1, replica_groups=mesh['row'=16,'col'=32] {'row'}, dimensions={0} | all-to-all | bytes 65536 | tf_op jit(solution)/shard_map/all_to_all | solution.py:14
  99.8 0.2 add_reduce_fusion.3
  100.1 0.6 exponential_reduce_fusion.3
  100.7 12.3 %all_to_all.54 = f32[32,8,128]{2,1,0:T(8,128)S(1)} all-to-all(f32[32,8,128]{2,1,0:T(8,128)S(1)} %broadcast_in_dim.20), channel_id=1, replica_groups=mesh['row'=16,'col'=32] {'col'}, dimensions={0} | all-to-all | bytes 262144 | tf_op jit(solution)/shard_map/all_to_all | solution.py:14
  113.0 0.2 add_reduce_fusion.2
  113.3 0.4 exponential_reduce_fusion.2
  113.7 12.0 %all_to_all.55 = f32[16,4,128]{2,1,0:T(4,128)S(1)} all-to-all(f32[16,4,128]{2,1,0:T(4,128)S(1)} %broadcast_in_dim.21), channel_id=1, replica_groups=mesh['row'=16,'col'=32] {'row'}, dimensions={0} | all-to-all | bytes 65536 | tf_op jit(solution)/shard_map/all_to_all | solution.py:14
  125.8 0.2 add_reduce_fusion.1
  126.0 0.6 exponential_reduce_fusion.1
  126.6 12.4 %all_to_all.56 = f32[32,8,128]{2,1,0:T(8,128)S(1)} all-to-all(f32[32,8,128]{2,1,0:T(8,128)S(1)} %broadcast_in_dim.22), channel_id=1, replica_groups=mesh['row'=16,'col'=32] {'col'}, dimensions={0} | all-to-all | bytes 262144 | tf_op jit(solution)/shard_map/all_to_all | solution.py:14
  139.1 0.0 copy-start.1
  139.1 0.2 add_reduce_fusion
  139.3 0.4 exponential_reduce_fusion
  139.8 12.0 %all_to_all.57 = f32[16,4,128]{2,1,0:T(4,128)S(1)} all-to-all(f32[16,4,128]{2,1,0:T(4,128)S(1)} %broadcast_in_dim.23), channel_id=1, replica_groups=mesh['row'=16,'col'=32] {'row'}, dimensions={0} | all-to-all | bytes 65536 | tf_op jit(solution)/shard_map/all_to_all | solution.py:14
  151.8 4.4 %fusion.4 = f32[512,256]{0,1:T(8,128)} fusion(f32[1024,512]{1,0:T(8,128)S(1)} %get-tuple-element.5, f32[32,8,1024]{2,1,0:T(8,128)} %copy-done, f32[512]{0:T(512)S(1)} %subtract_bitcast_fusion.3, f32[1024]{0:T(1024)S(1)} %subtract_bitcast_fusion), kind=kOutput, calls=%fused_computation.17 | convolution fusion | flops 1611792384 | bytes 3676160 | tf_op jit(solution)/shard_map/dot_general | solution.py:59
  156.3 3.8 %all-to-all-start.9 = ((f32[16,16,512]{2,1,0:T(8,128)}), f32[16,16,512]{2,1,0:T(8,128)S(1)}, u32[]{:S(2)}, u32[]{:S(2)}) async-start(f32[16,16,512]{2,1,0:T(8,128)} %bitcast.47), calls=%async_computation.9 | async-start | bytes 1048576 | tf_op jit(solution)/shard_map/all_to_all | solution.py:18
  160.0 3.3 %fusion.3 = f32[32,8,1024]{2,1,0:T(8,128)} fusion(f32[256,512]{1,0:T(8,128)S(1)} %bitcast.46, f32[1024,512]{1,0:T(8,128)S(1)} %get-tuple-element.5, f32[512]{0:T(512)S(1)} %subtract_bitcast_fusion.3, f32[1024]{0:T(1024)S(1)} %subtract_bitcast_fusion), kind=kOutput, calls=%fused_computation.16 | convolution fusion | flops 1611923456 | bytes 3676160 | tf_op jit(solution)/shard_map/dot_general | solution.py:69
  163.4 13.9 %all-to-all-done.9 = f32[16,16,512]{2,1,0:T(8,128)S(1)} async-done(((f32[16,16,512]{2,1,0:T(8,128)}), f32[16,16,512]{2,1,0:T(8,128)S(1)}, u32[]{:S(2)}, u32[]{:S(2)}) %all-to-all-start.9) | async-done | bytes 524320 | tf_op jit(solution)/shard_map/all_to_all | solution.py:18
  177.3 3.9 %all-to-all-start.8 = ((f32[32,8,1024]{2,1,0:T(8,128)}), f32[32,8,1024]{2,1,0:T(8,128)S(1)}, u32[]{:S(2)}, u32[]{:S(2)}) async-start(f32[32,8,1024]{2,1,0:T(8,128)} %fusion.3), calls=%async_computation.8 | async-start | bytes 2097152 | tf_op jit(solution)/shard_map/all_to_all | solution.py:18
  181.2 0.7 reduce_sum.139
  181.8 27.5 %all-to-all-done.8 = f32[32,8,1024]{2,1,0:T(8,128)S(1)} async-done(((f32[32,8,1024]{2,1,0:T(8,128)}), f32[32,8,1024]{2,1,0:T(8,128)S(1)}, u32[]{:S(2)}, u32[]{:S(2)}) %all-to-all-start.8) | async-done | bytes 1048608 | tf_op jit(solution)/shard_map/all_to_all | solution.py:18
  209.3 0.7 reduce_sum.138
  (34 shorter events, 0.6 us)
Async XLA Ops:
  68.8 1.0 copy-start
  139.1 20.9 %copy-start.1 = (f32[1024]{0:T(1024)}, f32[1024]{0:T(1024)S(1)}, u32[]{:S(2)}) copy-start(f32[1024]{0:T(1024)S(1)} %subtract_bitcast_fusion) | copy-start | bytes 12292
  151.8 8.2 %copy-start.2 = (f32[512]{0:T(512)}, f32[512]{0:T(512)S(1)}, u32[]{:S(2)}) copy-start(f32[512]{0:T(512)S(1)} %subtract_bitcast_fusion.3) | copy-start | bytes 6148
  156.3 21.0 %all-to-all-start.9 = ((f32[16,16,512]{2,1,0:T(8,128)}), f32[16,16,512]{2,1,0:T(8,128)S(1)}, u32[]{:S(2)}, u32[]{:S(2)}) async-start(f32[16,16,512]{2,1,0:T(8,128)} %bitcast.47), calls=%async_computation.9 | async-start | bytes 1048576 | tf_op jit(solution)/shard_map/all_to_all | solution.py:18
  177.3 32.1 %all-to-all-start.8 = ((f32[32,8,1024]{2,1,0:T(8,128)}), f32[32,8,1024]{2,1,0:T(8,128)S(1)}, u32[]{:S(2)}, u32[]{:S(2)}) async-start(f32[32,8,1024]{2,1,0:T(8,128)} %fusion.3), calls=%async_computation.8 | async-start | bytes 2097152 | tf_op jit(solution)/shard_map/all_to_all | solution.py:18

commit v2 on v1

v2 whole, which is shorter than its diff:
```python
import math

import jax
import jax.numpy as jnp
from jax import lax
from jax.sharding import PartitionSpec as P


ITERS = 3
LANES = 128


def spread(block, axis):
    n = lax.axis_size(axis)
    return lax.all_to_all(jnp.broadcast_to(block[None], (n,) + block.shape), axis, 0, 0)


def swap(chunks, axis):
    return lax.all_to_all(chunks, axis, 0, 0)


def fold(chunks, axis):
    me = lax.axis_index(axis).astype(jnp.uint32)
    n = chunks.shape[0]
    step = 1
    while n > 1:
        pairs = chunks.reshape((n // 2, 2) + chunks.shape[1:])
        bit = (me >> (step.bit_length() - 1)) & 1
        mine = lax.dynamic_index_in_dim(pairs, bit, 1, keepdims=False)
        other = lax.dynamic_index_in_dim(pairs, 1 - bit, 1, keepdims=False)
        partner = [(k, k ^ step) for k in range(lax.axis_size(axis))]
        chunks = mine + lax.ppermute(other, axis, partner)
        n, step = n // 2, step * 2
    return chunks[0]


def lse(values, dim):
    peak = jnp.max(values, axis=dim, keepdims=True)
    total = jnp.sum(jnp.exp(values - peak), axis=dim)
    return jnp.squeeze(peak, dim) + jnp.log(total)


def shared_lse(partial, axis):
    parts = spread(partial.reshape(-1, LANES), axis)
    return lse(parts, 0).reshape(partial.shape)


def gather_parts(graph_part, conf_part):
    graph_t = spread(graph_part, "col")
    conf_t = lax.all_gather(conf_part, "row")
    return graph_t.reshape(-1, graph_part.shape[1]), conf_t.reshape(-1, conf_part.shape[1])


def matmul(lhs, rhs, contract):
    return lax.dot_general(
        lhs,
        rhs,
        (contract, ((), ())),
        precision=lax.Precision.HIGHEST,
        preferred_element_type=jnp.float32,
    )


def steps(graph_emb, conf_emb):
    graph_t, conf_t = gather_parts(graph_emb.T, conf_emb.T)
    width, rows = graph_t.shape
    cols = conf_t.shape[1]
    batch = rows * lax.axis_size("row")
    scale = width ** (-0.5)
    score = matmul(graph_t, conf_t, ((0,), (0,))) * scale
    log_weight = -math.log(batch)
    row_pot = jnp.zeros((rows,), jnp.float32)
    col_pot = jnp.zeros((cols,), jnp.float32)
    for _ in range(ITERS):
        row_pot = log_weight - shared_lse(lse(col_pot[None, :] + score, 1), "col")
        col_pot = log_weight - shared_lse(lse(row_pot[:, None] + score, 0), "row")
    plan = jnp.exp(row_pot[:, None] + col_pot[None, :] + score)
    factor = -batch * scale
    graph_term = matmul(conf_t, plan, ((1,), (1,))) * factor
    graph_parts = swap(graph_term.reshape(lax.axis_size("col"), -1, rows), "col")
    conf_term = matmul(graph_t, plan, ((1,), (0,))) * factor
    grad_conf = fold(conf_term.reshape(lax.axis_size("row"), -1, cols), "row").T
    grad_graph = jnp.sum(graph_parts, axis=0).T
    return (grad_graph, grad_conf, row_pot, col_pot)


def solution(mesh):
    return jax.shard_map(
        steps,
        mesh=mesh,
        in_specs=(P("row", "col"), P("col", "row")),
        out_specs=(P("row", "col"), P("col", "row"), P("row"), P("col")),
        check_vma=False,
    )
```

time: 211 us -> 178 us (0.84); the launches traced: 210 us -> 175 us
  blocking collectives: 142 us -> 99.1 us
  starting transfers between devices: 7.68 us -> 28.7 us
  waiting for transfers between devices: 41.4 us -> 24.3 us
    all_to_all x8 -> x5, blocking collectives: 142 us -> 73.7 us  [spread(): lax.all_to_all(jnp.broadcast_to(block[None], (n,) + block.shape), axis, 0...]
    all_to_all x2 -> x1, waiting for transfers between devices: 41.4 us -> 0.01 us  [swap(): return lax.all_to_all(chunks, axis, 0, 0)]
    all_gather x0 -> x1, blocking collectives: none -> 25.4 us  [gather_parts(): conf_t = lax.all_gather(conf_part, 'row')]
    ppermute x0 -> x4, waiting for transfers between devices: none -> 16.8 us  [fold(): chunks = mine + lax.ppermute(other, axis, partner)]
    all_to_all x0 -> x2, starting transfers between devices: none -> 16 us  [spread(): lax.all_to_all(jnp.broadcast_to(block[None], (n,) + block.shape), axis, 0...]
    ppermute x0 -> x4, starting transfers between devices: none -> 8.59 us  [fold(): chunks = mine + lax.ppermute(other, axis, partner)]
    all_to_all x0 -> x2, waiting for transfers between devices: none -> 7.48 us  [spread(): lax.all_to_all(jnp.broadcast_to(block[None], (n,) + block.shape), axis, 0...]
    all_to_all x2 -> x1, starting transfers between devices: 7.68 us -> 4.11 us  [swap(): return lax.all_to_all(chunks, axis, 0, 0)]
  transfers between devices with their start and end apart: 2 -> 7, of which waited for: 2 -> 5; matrix products, arithmetic and copies ran while one was open for 2% -> 4% of each run, Pallas kernels for 0% -> 0%
where the time goes in v2:
time: 178 us; the launch traced here: 175 us
  blocking collectives  99.1 us (56%)
  starting transfers between devices  28.7 us (16%)
  waiting for transfers between devices  24.3 us (14%)
  matrix products  10.9 us (6%)
  other arithmetic  7.07 us (4%)
  local copies, waits for them, and re-layouts  3.61 us (2%)
    all_to_all x5, blocking collectives, spread(): lax.all_to_all(jnp.broadcast_to(block[None], (n,) + block.shape), axis, 0...  73.7 us
    all_gather x1, blocking collectives, gather_parts(): conf_t = lax.all_gather(conf_part, 'row')  25.4 us
    ppermute x4, waiting for transfers between devices, fold(): chunks = mine + lax.ppermute(other, axis, partner)  16.8 us
    all_to_all x2, starting transfers between devices, spread(): lax.all_to_all(jnp.broadcast_to(block[None], (n,) + block.shape), axis, 0...  16 us
    dot_general x3, matrix products, matmul(): lax.dot_general(lhs, rhs, (contract, ((), ())), precision=lax.Precision.H...  10.9 us
    ppermute x4, starting transfers between devices, fold(): chunks = mine + lax.ppermute(other, axis, partner)  8.59 us
    all_to_all x2, waiting for transfers between devices, spread(): lax.all_to_all(jnp.broadcast_to(block[None], (n,) + block.shape), axis, 0...  7.48 us
    all_to_all x1, starting transfers between devices, swap(): return lax.all_to_all(chunks, axis, 0, 0)  4.11 us
  transfers between devices with their start and end apart: 7, of which 5 were waited for; matrix products, arithmetic and copies ran while one was open for 4% of the time, Pallas kernels for 0%

profile of v2, /device:TPU:1, one launch (start us, length us, event | category | flops | bytes accessed | tf_op | source)
XLA Modules:
  0.0 174.6 jit_solution(3622147430537889961)
XLA Ops:
  0.6 1.9 %broadcast_in_dim.14 = f32[32,8,1024]{2,1,0:T(8,128)} broadcast(f32[8,1024]{1,0:T(8,128)} %bitcast.65), dimensions={1,2} | broadcast | bytes 1081344 | tf_op jit(solution)/shard_map/broadcast_in_dim | solution.py:15
  2.6 10.6 %all-to-all-start = ((f32[32,8,1024]{2,1,0:T(8,128)}), f32[32,8,1024]{2,1,0:T(8,128)}, u32[]{:S(2)}, u32[]{:S(2)}) async-start(f32[32,8,1024]{2,1,0:T(8,128)} %broadcast_in_dim.14), calls=%async_computation | async-start | bytes 2097152 | tf_op jit(solution)/shard_map/all_to_all | solution.py:15
  13.2 25.4 %all-gather = f32[256,512]{1,0:T(8,128)S(1)} all-gather(f32[16,512]{1,0:T(8,128)S(1)} %bitcast.66), channel_id=2, replica_groups=mesh['row'=16,'col'=32] {'row'}, dimensions={0}, use_global_device_ids=true | all-gather | bytes 557056 | tf_op jit(solution)/shard_map/all_gather | solution.py:50
  38.6 3.2 %fusion.11 = (f32[1024]{0:T(1024)S(1)}, f32[1024,512]{1,0:T(8,128)S(1)}) fusion(f32[256,512]{1,0:T(8,128)S(1)} %all-gather, f32[32,8,1024]{2,1,0:T(8,128)} %all-to-all-done), kind=kOutput, calls=%fused_computation.50 | convolution fusion | flops 1611660288 | bytes 3674112 | tf_op jit(solution)/shard_map/dot_general | solution.py:55
  41.8 0.7 exponential_reduce_fusion.5
  42.5 18.4 %all_to_all.40 = f32[32,8,128]{2,1,0:T(8,128)S(1)} all-to-all(f32[32,8,128]{2,1,0:T(8,128)S(1)} %broadcast_in_dim.15), channel_id=1, replica_groups=mesh['row'=16,'col'=32] {'col'}, dimensions={0} | all-to-all | bytes 262144 | tf_op jit(solution)/shard_map/all_to_all | solution.py:15
  61.2 0.4 exponential_reduce_fusion.4
  61.7 18.6 %all_to_all.41 = f32[16,4,128]{2,1,0:T(4,128)S(1)} all-to-all(f32[16,4,128]{2,1,0:T(4,128)S(1)} %broadcast_in_dim.16), channel_id=1, replica_groups=mesh['row'=16,'col'=32] {'row'}, dimensions={0} | all-to-all | bytes 65536 | tf_op jit(solution)/shard_map/all_to_all | solution.py:15
  80.5 0.6 exponential_reduce_fusion.3
  81.1 12.3 %all_to_all.42 = f32[32,8,128]{2,1,0:T(8,128)S(1)} all-to-all(f32[32,8,128]{2,1,0:T(8,128)S(1)} %broadcast_in_dim.17), channel_id=1, replica_groups=mesh['row'=16,'col'=32] {'col'}, dimensions={0} | all-to-all | bytes 262144 | tf_op jit(solution)/shard_map/all_to_all | solution.py:15
  93.8 0.4 exponential_reduce_fusion.2
  94.2 12.0 %all_to_all.43 = f32[16,4,128]{2,1,0:T(4,128)S(1)} all-to-all(f32[16,4,128]{2,1,0:T(4,128)S(1)} %broadcast_in_dim.18), channel_id=1, replica_groups=mesh['row'=16,'col'=32] {'row'}, dimensions={0} | all-to-all | bytes 65536 | tf_op jit(solution)/shard_map/all_to_all | solution.py:15
  106.5 0.6 exponential_reduce_fusion.1
  107.1 12.4 %all_to_all.44 = f32[32,8,128]{2,1,0:T(8,128)S(1)} all-to-all(f32[32,8,128]{2,1,0:T(8,128)S(1)} %broadcast_in_dim.19), channel_id=1, replica_groups=mesh['row'=16,'col'=32] {'col'}, dimensions={0} | all-to-all | bytes 262144 | tf_op jit(solution)/shard_map/all_to_all | solution.py:15
  120.3 0.6 broadcast_in_dim.20
  120.9 5.4 %all-to-all-start.6 = ((f32[16,4,128]{2,1,0:T(4,128)}), f32[16,4,128]{2,1,0:T(4,128)S(1)}, u32[]{:S(2)}, u32[]{:S(2)}) async-start(f32[16,4,128]{2,1,0:T(4,128)} %broadcast_in_dim.20), calls=%async_computation.6 | async-start | bytes 65536 | tf_op jit(solution)/shard_map/all_to_all | solution.py:15
  126.3 7.5 %all-to-all-done.6 = f32[16,4,128]{2,1,0:T(4,128)S(1)} async-done(((f32[16,4,128]{2,1,0:T(4,128)}), f32[16,4,128]{2,1,0:T(4,128)S(1)}, u32[]{:S(2)}, u32[]{:S(2)}) %all-to-all-start.6) | async-done | bytes 32800 | tf_op jit(solution)/shard_map/all_to_all | solution.py:15
  133.9 3.4 %fusion.3 = f32[32,8,1024]{2,1,0:T(8,128)} fusion(f32[256,512]{1,0:T(8,128)S(1)} %all-gather, f32[1024,512]{1,0:T(8,128)S(1)} %get-tuple-element.5, f32[512]{0:T(512)S(1)} %subtract_bitcast_fusion.3, f32[1024]{0:T(1024)S(1)} %subtract_bitcast_fusion), kind=kOutput, calls=%fused_computation.16 | convolution fusion | flops 1611923456 | bytes 3676160 | tf_op jit(solution)/shard_map/dot_general | solution.py:55
  137.2 4.1 %all-to-all-start.7 = ((f32[32,8,1024]{2,1,0:T(8,128)}), f32[32,8,1024]{2,1,0:T(8,128)S(1)}, u32[]{:S(2)}, u32[]{:S(2)}) async-start(f32[32,8,1024]{2,1,0:T(8,128)} %fusion.3), calls=%async_computation.7 | async-start | bytes 2097152 | tf_op jit(solution)/shard_map/all_to_all | solution.py:19
  141.4 4.4 %fusion.4 = f32[512,256]{0,1:T(8,128)} fusion(f32[1024,512]{1,0:T(8,128)S(1)} %get-tuple-element.5, f32[32,8,1024]{2,1,0:T(8,128)} %all-to-all-done, f32[512]{0:T(512)S(1)} %subtract_bitcast_fusion.3, f32[1024]{0:T(1024)S(1)} %subtract_bitcast_fusion), kind=kOutput, calls=%fused_computation.17 | convolution fusion | flops 1611792384 | bytes 3676160 | tf_op jit(solution)/shard_map/dot_general | solution.py:55
  145.8 1.0 dynamic-slice_bitcast_fusion
  146.8 2.3 %collective-permute-start = (f32[8,16,512]{2,1,0:T(8,128)S(1)}, f32[8,16,512]{2,1,0:T(8,128)S(1)}, u32[]{:S(2)}, u32[]{:S(2)}) collective-permute-start(f32[8,16,512]{2,1,0:T(8,128)S(1)} %dynamic-slice_bitcast_fusion), channel_id=1, source_target_pairs={{0,32},{32,0},{64,96},{96,64},{128,160},{160,128},{192,224},{224,1... | collective-permute-start | bytes 786440 | tf_op jit(solution)/shard_map/ppermute | solution.py:32
  149.1 1.1 collective-permute-done
  150.2 1.0 bitcast_add_fusion
  151.2 2.1 %collective-permute-start.1 = (f32[4,16,512]{2,1,0:T(8,128)S(1)}, f32[4,16,512]{2,1,0:T(8,128)S(1)}, u32[]{:S(2)}, u32[]{:S(2)}) collective-permute-start(f32[4,16,512]{2,1,0:T(8,128)S(1)} %dynamic-slice_bitcast_fusion.1), channel_id=1, source_target_pairs={{0,64},{32,96},{64,0},{96,32},{128,192},{160,224},{192,128},{224,1... | collective-permute-start | bytes 393224 | tf_op jit(solution)/shard_map/ppermute | solution.py:32
  153.4 4.4 %collective-permute-done.1 = f32[4,16,512]{2,1,0:T(8,128)S(1)} collective-permute-done((f32[4,16,512]{2,1,0:T(8,128)S(1)}, f32[4,16,512]{2,1,0:T(8,128)S(1)}, u32[]{:S(2)}, u32[]{:S(2)}) %collective-permute-start.1) | collective-permute-done | bytes 131104 | tf_op jit(solution)/shard_map/ppermute | solution.py:32
  157.8 2.2 %collective-permute-start.2 = (f32[2,16,512]{2,1,0:T(8,128)S(1)}, f32[2,16,512]{2,1,0:T(8,128)S(1)}, u32[]{:S(2)}, u32[]{:S(2)}) collective-permute-start(f32[2,16,512]{2,1,0:T(8,128)S(1)} %dynamic-slice_bitcast_fusion.2), channel_id=1, source_target_pairs={{0,128},{32,160},{64,192},{96,224},{128,0},{160,32},{192,64},{224,... | collective-permute-start | bytes 196616 | tf_op jit(solution)/shard_map/ppermute | solution.py:32
  160.1 4.6 %collective-permute-done.2 = f32[2,16,512]{2,1,0:T(8,128)S(1)} collective-permute-done((f32[2,16,512]{2,1,0:T(8,128)S(1)}, f32[2,16,512]{2,1,0:T(8,128)S(1)}, u32[]{:S(2)}, u32[]{:S(2)}) %collective-permute-start.2) | collective-permute-done | bytes 65568 | tf_op jit(solution)/shard_map/ppermute | solution.py:32
  164.7 1.9 %collective-permute-start.3 = (f32[1,16,512]{2,1,0:T(8,128)S(1)}, f32[1,16,512]{2,1,0:T(8,128)S(1)}, u32[]{:S(2)}, u32[]{:S(2)}) collective-permute-start(f32[1,16,512]{2,1,0:T(8,128)S(1)} %constant_dynamic-slice_fusion), channel_id=1, source_target_pairs={{0,256},{32,288},{64,320},{96,352},{128,384},{160,416},{192,448},{... | collective-permute-start | bytes 98312 | tf_op jit(solution)/shard_map/ppermute | solution.py:32
  166.7 6.7 %collective-permute-done.3 = f32[1,16,512]{2,1,0:T(8,128)S(1)} collective-permute-done((f32[1,16,512]{2,1,0:T(8,128)S(1)}, f32[1,16,512]{2,1,0:T(8,128)S(1)}, u32[]{:S(2)}, u32[]{:S(2)}) %collective-permute-start.3) | collective-permute-done | bytes 32800 | tf_op jit(solution)/shard_map/ppermute | solution.py:32
  173.3 0.6 add_bitcast_fusion
  173.9 0.7 reduce_sum.129
  (48 shorter events, 2.2 us)
Async XLA Ops:
  0.6 12.6 %copy-start.1 = (f32[512,16]{0,1:T(8,128)S(1)}, f32[512,16]{0,1:T(8,128)}, u32[]{:S(2)}) copy-start(f32[512,16]{0,1:T(8,128)} %param.3) | copy-start | bytes 98308
  2.6 36.0 %all-to-all-start = ((f32[32,8,1024]{2,1,0:T(8,128)}), f32[32,8,1024]{2,1,0:T(8,128)}, u32[]{:S(2)}, u32[]{:S(2)}) async-start(f32[32,8,1024]{2,1,0:T(8,128)} %broadcast_in_dim.14), calls=%async_computation | async-start | bytes 2097152 | tf_op jit(solution)/shard_map/all_to_all | solution.py:15
  119.6 21.7 %copy-start = (f32[1024]{0:T(1024)}, f32[1024]{0:T(1024)S(1)}, u32[]{:S(2)}) copy-start(f32[1024]{0:T(1024)S(1)} %subtract_bitcast_fusion) | copy-start | bytes 12292
  120.9 12.9 %all-to-all-start.6 = ((f32[16,4,128]{2,1,0:T(4,128)}), f32[16,4,128]{2,1,0:T(4,128)S(1)}, u32[]{:S(2)}, u32[]{:S(2)}) async-start(f32[16,4,128]{2,1,0:T(4,128)} %broadcast_in_dim.20), calls=%async_computation.6 | async-start | bytes 65536 | tf_op jit(solution)/shard_map/all_to_all | solution.py:15
  133.9 7.5 %copy-start.2 = (f32[512]{0:T(512)}, f32[512]{0:T(512)S(1)}, u32[]{:S(2)}) copy-start(f32[512]{0:T(512)S(1)} %subtract_bitcast_fusion.3) | copy-start | bytes 6148
  137.2 36.7 %all-to-all-start.7 = ((f32[32,8,1024]{2,1,0:T(8,128)}), f32[32,8,1024]{2,1,0:T(8,128)S(1)}, u32[]{:S(2)}, u32[]{:S(2)}) async-start(f32[32,8,1024]{2,1,0:T(8,128)} %fusion.3), calls=%async_computation.7 | async-start | bytes 2097152 | tf_op jit(solution)/shard_map/all_to_all | solution.py:19
  146.8 3.5 %collective-permute-start = (f32[8,16,512]{2,1,0:T(8,128)S(1)}, f32[8,16,512]{2,1,0:T(8,128)S(1)}, u32[]{:S(2)}, u32[]{:S(2)}) collective-permute-start(f32[8,16,512]{2,1,0:T(8,128)S(1)} %dynamic-slice_bitcast_fusion), channel_id=1, source_target_pairs={{0,32},{32,0},{64,96},{96,64},{128,160},{160,128},{192,224},{224,1... | collective-permute-start | bytes 786440 | tf_op jit(solution)/shard_map/ppermute | solution.py:32
  151.2 6.6 %collective-permute-start.1 = (f32[4,16,512]{2,1,0:T(8,128)S(1)}, f32[4,16,512]{2,1,0:T(8,128)S(1)}, u32[]{:S(2)}, u32[]{:S(2)}) collective-permute-start(f32[4,16,512]{2,1,0:T(8,128)S(1)} %dynamic-slice_bitcast_fusion.1), channel_id=1, source_target_pairs={{0,64},{32,96},{64,0},{96,32},{128,192},{160,224},{192,128},{224,1... | collective-permute-start | bytes 393224 | tf_op jit(solution)/shard_map/ppermute | solution.py:32
  157.8 6.9 %collective-permute-start.2 = (f32[2,16,512]{2,1,0:T(8,128)S(1)}, f32[2,16,512]{2,1,0:T(8,128)S(1)}, u32[]{:S(2)}, u32[]{:S(2)}) collective-permute-start(f32[2,16,512]{2,1,0:T(8,128)S(1)} %dynamic-slice_bitcast_fusion.2), channel_id=1, source_target_pairs={{0,128},{32,160},{64,192},{96,224},{128,0},{160,32},{192,64},{224,... | collective-permute-start | bytes 196616 | tf_op jit(solution)/shard_map/ppermute | solution.py:32
  164.7 8.6 %collective-permute-start.3 = (f32[1,16,512]{2,1,0:T(8,128)S(1)}, f32[1,16,512]{2,1,0:T(8,128)S(1)}, u32[]{:S(2)}, u32[]{:S(2)}) collective-permute-start(f32[1,16,512]{2,1,0:T(8,128)S(1)} %constant_dynamic-slice_fusion), channel_id=1, source_target_pairs={{0,256},{32,288},{64,320},{96,352},{128,384},{160,416},{192,448},{... | collective-permute-start | bytes 98312 | tf_op jit(solution)/shard_map/ppermute | solution.py:32

commit v3 on v2

--- a/solution.py
+++ b/solution.py
@@ -21,16 +21,17 @@
 
 def fold(chunks, axis):
     me = lax.axis_index(axis).astype(jnp.uint32)
-    n = chunks.shape[0]
-    step = 1
+    n, shift = chunks.shape[0], 0
     while n > 1:
-        pairs = chunks.reshape((n // 2, 2) + chunks.shape[1:])
-        bit = (me >> (step.bit_length() - 1)) & 1
-        mine = lax.dynamic_index_in_dim(pairs, bit, 1, keepdims=False)
-        other = lax.dynamic_index_in_dim(pairs, 1 - bit, 1, keepdims=False)
-        partner = [(k, k ^ step) for k in range(lax.axis_size(axis))]
-        chunks = mine + lax.ppermute(other, axis, partner)
-        n, step = n // 2, step * 2
+        radix = n if n <= 4 else 2
+        groups = chunks.reshape((n // radix, radix) + chunks.shape[1:])
+        digit = (me >> shift) & (radix - 1)
+        chunks = lax.dynamic_index_in_dim(groups, digit, 1, keepdims=False)
+        for d in range(1, radix):
+            sent = lax.dynamic_index_in_dim(groups, digit ^ d, 1, keepdims=False)
+            partner = [(k, k ^ (d << shift)) for k in range(lax.axis_size(axis))]
+            chunks = chunks + lax.ppermute(sent, axis, partner)
+        n, shift = n // radix, shift + radix.bit_length() - 1
     return chunks[0]
 
 
@@ -51,12 +52,12 @@
     return graph_t.reshape(-1, graph_part.shape[1]), conf_t.reshape(-1, conf_part.shape[1])
 
 
-def matmul(lhs, rhs, contract):
+def matmul(lhs, rhs, contract, precision):
     return lax.dot_general(
         lhs,
         rhs,
         (contract, ((), ())),
-        precision=lax.Precision.HIGHEST,
+        precision=precision,
         preferred_element_type=jnp.float32,
     )
 
@@ -67,7 +68,7 @@
     cols = conf_t.shape[1]
     batch = rows * lax.axis_size("row")
     scale = width ** (-0.5)
-    score = matmul(graph_t, conf_t, ((0,), (0,))) * scale
+    score = matmul(graph_t, conf_t, ((0,), (0,)), lax.Precision.HIGHEST) * scale
     log_weight = -math.log(batch)
     row_pot = jnp.zeros((rows,), jnp.float32)
     col_pot = jnp.zeros((cols,), jnp.float32)
@@ -76,9 +77,9 @@
         col_pot = log_weight - shared_lse(lse(row_pot[:, None] + score, 0), "row")
     plan = jnp.exp(row_pot[:, None] + col_pot[None, :] + score)
     factor = -batch * scale
-    graph_term = matmul(conf_t, plan, ((1,), (1,))) * factor
+    graph_term = matmul(conf_t, plan, ((1,), (1,)), lax.Precision.HIGH) * factor
     graph_parts = swap(graph_term.reshape(lax.axis_size("col"), -1, rows), "col")
-    conf_term = matmul(graph_t, plan, ((1,), (0,))) * factor
+    conf_term = matmul(graph_t, plan, ((1,), (0,)), lax.Precision.HIGH) * factor
     grad_conf = fold(conf_term.reshape(lax.axis_size("row"), -1, cols), "row").T
     grad_graph = jnp.sum(graph_parts, axis=0).T
     return (grad_graph, grad_conf, row_pot, col_pot)

time: 178 us -> 170 us (0.955)
  waiting for transfers between devices: 24.3 us -> 7.88 us
  blocking collectives: 99.1 us -> 111 us
  matrix products: 10.9 us -> 8.04 us
    all_to_all x5 -> x6, blocking collectives: 73.7 us -> 85.6 us  [spread(): lax.all_to_all(jnp.broadcast_to(block[None], (n,) + block.shape), axis, 0...]
    ppermute x4 -> x5, waiting for transfers between devices: 16.8 us -> 7.88 us  [fold(): chunks = chunks + lax.ppermute(sent, axis, partner)]
    all_to_all x2 -> x1, waiting for transfers between devices: 7.48 us -> 0.01 us  [spread(): lax.all_to_all(jnp.broadcast_to(block[None], (n,) + block.shape), axis, 0...]
    ppermute x4 -> x5, starting transfers between devices: 8.59 us -> 15.8 us  [fold(): chunks = chunks + lax.ppermute(sent, axis, partner)]
    all_to_all x2 -> x1, starting transfers between devices: 16 us -> 10.6 us  [spread(): lax.all_to_all(jnp.broadcast_to(block[None], (n,) + block.shape), axis, 0...]
    dot_general x3, matrix products: 10.9 us -> 8.04 us  [matmul(): lax.dot_general(lhs, rhs, (contract, ((), ())), precision=precision, pref...]
  transfers between devices with their start and end apart: 7 -> 7, of which waited for: 5 -> 3; matrix products, arithmetic and copies ran while one was open for 4% -> 3% of each run, Pallas kernels for 0% -> 0%
where the time goes in v3:
time: 170 us; the launch traced here: 168 us
  blocking collectives  111 us (65%)
  starting transfers between devices  30.4 us (18%)
  matrix products  8.04 us (5%)
  waiting for transfers between devices  7.88 us (5%)
  other arithmetic  7.07 us (4%)
  local copies, waits for them, and re-layouts  2.8 us (2%)
    all_to_all x6, blocking collectives, spread(): lax.all_to_all(jnp.broadcast_to(block[None], (n,) + block.shape), axis, 0...  85.6 us
    all_gather x1, blocking collectives, gather_parts(): conf_t = lax.all_gather(conf_part, 'row')  25.4 us
    ppermute x5, starting transfers between devices, fold(): chunks = chunks + lax.ppermute(sent, axis, partner)  15.8 us
    all_to_all x1, starting transfers between devices, spread(): lax.all_to_all(jnp.broadcast_to(block[None], (n,) + block.shape), axis, 0...  10.6 us
    dot_general x3, matrix products, matmul(): lax.dot_general(lhs, rhs, (contract, ((), ())), precision=precision, pref...  8.04 us
    ppermute x5, waiting for transfers between devices, fold(): chunks = chunks + lax.ppermute(sent, axis, partner)  7.88 us
    all_to_all x1, starting transfers between devices, swap(): return lax.all_to_all(chunks, axis, 0, 0)  3.93 us
  transfers between devices with their start and end apart: 7, of which 3 were waited for; matrix products, arithmetic and copies ran while one was open for 3% of the time, Pallas kernels for 0%

profile of v3, /device:TPU:1, one launch (start us, length us, event | category | flops | bytes accessed | tf_op | source)
XLA Modules:
  0.0 168.1 jit_solution(3845502440329296676)
XLA Ops:
  0.6 1.9 %broadcast_in_dim.14 = f32[32,8,1024]{2,1,0:T(8,128)} broadcast(f32[8,1024]{1,0:T(8,128)} %bitcast.60), dimensions={1,2} | broadcast | bytes 1081344 | tf_op jit(solution)/shard_map/broadcast_in_dim | solution.py:15
  2.5 10.6 %all-to-all-start = ((f32[32,8,1024]{2,1,0:T(8,128)}), f32[32,8,1024]{2,1,0:T(8,128)}, u32[]{:S(2)}, u32[]{:S(2)}) async-start(f32[32,8,1024]{2,1,0:T(8,128)} %broadcast_in_dim.14), calls=%async_computation | async-start | bytes 2097152 | tf_op jit(solution)/shard_map/all_to_all | solution.py:15
  13.1 25.4 %all-gather = f32[256,512]{1,0:T(8,128)S(1)} all-gather(f32[16,512]{1,0:T(8,128)S(1)} %bitcast.61), channel_id=2, replica_groups=mesh['row'=16,'col'=32] {'row'}, dimensions={0}, use_global_device_ids=true | all-gather | bytes 557056 | tf_op jit(solution)/shard_map/all_gather | solution.py:51
  38.5 3.2 %fusion.11 = (f32[1024]{0:T(1024)S(1)}, f32[1024,512]{1,0:T(8,128)S(1)}) fusion(f32[256,512]{1,0:T(8,128)S(1)} %all-gather, f32[32,8,1024]{2,1,0:T(8,128)} %all-to-all-done), kind=kOutput, calls=%fused_computation.50 | convolution fusion | flops 1611660288 | bytes 3674112 | tf_op jit(solution)/shard_map/dot_general | solution.py:56
  41.7 0.7 exponential_reduce_fusion.5
  42.5 18.4 %all_to_all.40 = f32[32,8,128]{2,1,0:T(8,128)S(1)} all-to-all(f32[32,8,128]{2,1,0:T(8,128)S(1)} %broadcast_in_dim.15), channel_id=1, replica_groups=mesh['row'=16,'col'=32] {'col'}, dimensions={0} | all-to-all | bytes 262144 | tf_op jit(solution)/shard_map/all_to_all | solution.py:15
  61.2 0.4 exponential_reduce_fusion.4
  61.6 18.6 %all_to_all.41 = f32[16,4,128]{2,1,0:T(4,128)S(1)} all-to-all(f32[16,4,128]{2,1,0:T(4,128)S(1)} %broadcast_in_dim.16), channel_id=1, replica_groups=mesh['row'=16,'col'=32] {'row'}, dimensions={0} | all-to-all | bytes 65536 | tf_op jit(solution)/shard_map/all_to_all | solution.py:15
  80.5 0.6 exponential_reduce_fusion.3
  81.1 12.3 %all_to_all.42 = f32[32,8,128]{2,1,0:T(8,128)S(1)} all-to-all(f32[32,8,128]{2,1,0:T(8,128)S(1)} %broadcast_in_dim.17), channel_id=1, replica_groups=mesh['row'=16,'col'=32] {'col'}, dimensions={0} | all-to-all | bytes 262144 | tf_op jit(solution)/shard_map/all_to_all | solution.py:15
  93.5 0.2 add_reduce_fusion.2
  93.7 0.4 exponential_reduce_fusion.2
  94.2 12.0 %all_to_all.43 = f32[16,4,128]{2,1,0:T(4,128)S(1)} all-to-all(f32[16,4,128]{2,1,0:T(4,128)S(1)} %broadcast_in_dim.18), channel_id=1, replica_groups=mesh['row'=16,'col'=32] {'row'}, dimensions={0} | all-to-all | bytes 65536 | tf_op jit(solution)/shard_map/all_to_all | solution.py:15
  106.5 0.6 exponential_reduce_fusion.1
  107.1 12.4 %all_to_all.44 = f32[32,8,128]{2,1,0:T(8,128)S(1)} all-to-all(f32[32,8,128]{2,1,0:T(8,128)S(1)} %broadcast_in_dim.19), channel_id=1, replica_groups=mesh['row'=16,'col'=32] {'col'}, dimensions={0} | all-to-all | bytes 262144 | tf_op jit(solution)/shard_map/all_to_all | solution.py:15
  119.8 0.4 exponential_reduce_fusion
  120.3 12.0 %all_to_all.45 = f32[16,4,128]{2,1,0:T(4,128)S(1)} all-to-all(f32[16,4,128]{2,1,0:T(4,128)S(1)} %broadcast_in_dim.20), channel_id=1, replica_groups=mesh['row'=16,'col'=32] {'row'}, dimensions={0} | all-to-all | bytes 65536 | tf_op jit(solution)/shard_map/all_to_all | solution.py:15
  132.3 2.3 %fusion.3 = f32[32,8,1024]{2,1,0:T(8,128)} fusion(f32[256,512]{1,0:T(8,128)S(1)} %all-gather, f32[1024,512]{1,0:T(8,128)S(1)} %get-tuple-element.8, f32[512]{0:T(512)S(1)} %subtract_bitcast_fusion.3, f32[1024]{0:T(1024)S(1)} %subtract_bitcast_fusion), kind=kOutput, calls=%fused_computation.16 | convolution fusion | flops 806617088 | bytes 3676160 | tf_op jit(solution)/shard_map/dot_general | solution.py:56
  134.6 3.9 %all-to-all-start.7 = ((f32[32,8,1024]{2,1,0:T(8,128)}), f32[32,8,1024]{2,1,0:T(8,128)S(1)}, u32[]{:S(2)}, u32[]{:S(2)}) async-start(f32[32,8,1024]{2,1,0:T(8,128)} %fusion.3), calls=%async_computation.7 | async-start | bytes 2097152 | tf_op jit(solution)/shard_map/all_to_all | solution.py:19
  138.6 2.6 %fusion.4 = f32[512,256]{0,1:T(8,128)S(1)} fusion(f32[1024,512]{1,0:T(8,128)S(1)} %get-tuple-element.8, f32[32,8,1024]{2,1,0:T(8,128)} %all-to-all-done, f32[512]{0:T(512)S(1)} %subtract_bitcast_fusion.3, f32[1024]{0:T(1024)S(1)} %subtract_bitcast_fusion), kind=kOutput, calls=%fused_computation.17 | convolution fusion | flops 806486016 | bytes 3676160 | tf_op jit(solution)/shard_map/dot_general | solution.py:56
  141.2 0.8 copy-done
  142.0 2.3 %collective-permute-start = (f32[8,16,512]{2,1,0:T(8,128)S(1)}, f32[8,16,512]{2,1,0:T(8,128)S(1)}, u32[]{:S(2)}, u32[]{:S(2)}) collective-permute-start(f32[8,16,512]{2,1,0:T(8,128)S(1)} %dynamic-slice_bitcast_fusion), channel_id=1, source_target_pairs={{0,32},{32,0},{64,96},{96,64},{128,160},{160,128},{192,224},{224,1... | collective-permute-start | bytes 786440 | tf_op jit(solution)/shard_map/ppermute | solution.py:33
  144.3 1.1 collective-permute-done
  145.4 1.0 bitcast_add_fusion
  146.5 2.1 %collective-permute-start.1 = (f32[4,16,512]{2,1,0:T(8,128)S(1)}, f32[4,16,512]{2,1,0:T(8,128)S(1)}, u32[]{:S(2)}, u32[]{:S(2)}) collective-permute-start(f32[4,16,512]{2,1,0:T(8,128)S(1)} %dynamic-slice_bitcast_fusion.1), channel_id=1, source_target_pairs={{0,64},{32,96},{64,0},{96,32},{128,192},{160,224},{192,128},{224,1... | collective-permute-start | bytes 393224 | tf_op jit(solution)/shard_map/ppermute | solution.py:33
  148.6 4.4 %collective-permute-done.1 = f32[4,16,512]{2,1,0:T(8,128)S(1)} collective-permute-done((f32[4,16,512]{2,1,0:T(8,128)S(1)}, f32[4,16,512]{2,1,0:T(8,128)S(1)}, u32[]{:S(2)}, u32[]{:S(2)}) %collective-permute-start.1) | collective-permute-done | bytes 131104 | tf_op jit(solution)/shard_map/ppermute | solution.py:33
  153.1 2.2 %collective-permute-start.2 = (f32[1,16,512]{2,1,0:T(8,128)S(1)}, f32[1,16,512]{2,1,0:T(8,128)S(1)}, u32[]{:S(2)}, u32[]{:S(2)}) collective-permute-start(f32[1,16,512]{2,1,0:T(8,128)S(1)} %get-tuple-element.4), channel_id=1, source_target_pairs={{0,128},{32,160},{64,192},{96,224},{128,0},{160,32},{192,64},{224,... | collective-permute-start | bytes 98312 | tf_op jit(solution)/shard_map/ppermute | solution.py:33
  155.3 3.9 %collective-permute-start.3 = (f32[1,16,512]{2,1,0:T(8,128)S(1)}, f32[1,16,512]{2,1,0:T(8,128)S(1)}, u32[]{:S(2)}, u32[]{:S(2)}) collective-permute-start(f32[1,16,512]{2,1,0:T(8,128)S(1)} %get-tuple-element.6), channel_id=1, source_target_pairs={{0,256},{32,288},{64,320},{96,352},{128,384},{160,416},{192,448},{... | collective-permute-start | bytes 98312 | tf_op jit(solution)/shard_map/ppermute | solution.py:33
  159.3 5.2 %collective-permute-start.4 = (f32[1,16,512]{2,1,0:T(8,128)S(1)}, f32[1,16,512]{2,1,0:T(8,128)S(1)}, u32[]{:S(2)}, u32[]{:S(2)}) collective-permute-start(f32[1,16,512]{2,1,0:T(8,128)S(1)} %get-tuple-element.5), channel_id=1, source_target_pairs={{0,384},{32,416},{64,448},{96,480},{128,256},{160,288},{192,320},{... | collective-permute-start | bytes 98312 | tf_op jit(solution)/shard_map/ppermute | solution.py:33
  164.5 2.3 %collective-permute-done.4 = f32[1,16,512]{2,1,0:T(8,128)S(1)} collective-permute-done((f32[1,16,512]{2,1,0:T(8,128)S(1)}, f32[1,16,512]{2,1,0:T(8,128)S(1)}, u32[]{:S(2)}, u32[]{:S(2)}) %collective-permute-start.4) | collective-permute-done | bytes 32800 | tf_op jit(solution)/shard_map/ppermute | solution.py:33
  166.8 0.6 add_bitcast_fusion
  167.4 0.7 reduce_sum.129
  (49 shorter events, 1.6 us)
Async XLA Ops:
  0.6 12.5 %copy-start.2 = (f32[512,16]{0,1:T(8,128)S(1)}, f32[512,16]{0,1:T(8,128)}, u32[]{:S(2)}) copy-start(f32[512,16]{0,1:T(8,128)} %param.3) | copy-start | bytes 98308
  2.5 36.0 %all-to-all-start = ((f32[32,8,1024]{2,1,0:T(8,128)}), f32[32,8,1024]{2,1,0:T(8,128)}, u32[]{:S(2)}, u32[]{:S(2)}) async-start(f32[32,8,1024]{2,1,0:T(8,128)} %broadcast_in_dim.14), calls=%async_computation | async-start | bytes 2097152 | tf_op jit(solution)/shard_map/all_to_all | solution.py:15
  119.6 19.0 %copy-start.1 = (f32[1024]{0:T(1024)}, f32[1024]{0:T(1024)S(1)}, u32[]{:S(2)}) copy-start(f32[1024]{0:T(1024)S(1)} %subtract_bitcast_fusion) | copy-start | bytes 12292
  132.3 6.3 %copy-start.3 = (f32[512]{0:T(512)}, f32[512]{0:T(512)S(1)}, u32[]{:S(2)}) copy-start(f32[512]{0:T(512)S(1)} %subtract_bitcast_fusion.3) | copy-start | bytes 6148
  134.6 32.8 %all-to-all-start.7 = ((f32[32,8,1024]{2,1,0:T(8,128)}), f32[32,8,1024]{2,1,0:T(8,128)S(1)}, u32[]{:S(2)}, u32[]{:S(2)}) async-start(f32[32,8,1024]{2,1,0:T(8,128)} %fusion.3), calls=%async_computation.7 | async-start | bytes 2097152 | tf_op jit(solution)/shard_map/all_to_all | solution.py:19
  141.1 0.8 copy-start
  142.0 3.5 %collective-permute-start = (f32[8,16,512]{2,1,0:T(8,128)S(1)}, f32[8,16,512]{2,1,0:T(8,128)S(1)}, u32[]{:S(2)}, u32[]{:S(2)}) collective-permute-start(f32[8,16,512]{2,1,0:T(8,128)S(1)} %dynamic-slice_bitcast_fusion), channel_id=1, source_target_pairs={{0,32},{32,0},{64,96},{96,64},{128,160},{160,128},{192,224},{224,1... | collective-permute-start | bytes 786440 | tf_op jit(solution)/shard_map/ppermute | solution.py:33
  146.5 6.6 %collective-permute-start.1 = (f32[4,16,512]{2,1,0:T(8,128)S(1)}, f32[4,16,512]{2,1,0:T(8,128)S(1)}, u32[]{:S(2)}, u32[]{:S(2)}) collective-permute-start(f32[4,16,512]{2,1,0:T(8,128)S(1)} %dynamic-slice_bitcast_fusion.1), channel_id=1, source_target_pairs={{0,64},{32,96},{64,0},{96,32},{128,192},{160,224},{192,128},{224,1... | collective-permute-start | bytes 393224 | tf_op jit(solution)/shard_map/ppermute | solution.py:33
  153.1 11.4 %collective-permute-start.2 = (f32[1,16,512]{2,1,0:T(8,128)S(1)}, f32[1,16,512]{2,1,0:T(8,128)S(1)}, u32[]{:S(2)}, u32[]{:S(2)}) collective-permute-start(f32[1,16,512]{2,1,0:T(8,128)S(1)} %get-tuple-element.4), channel_id=1, source_target_pairs={{0,128},{32,160},{64,192},{96,224},{128,0},{160,32},{192,64},{224,... | collective-permute-start | bytes 98312 | tf_op jit(solution)/shard_map/ppermute | solution.py:33
  155.3 9.2 %collective-permute-start.3 = (f32[1,16,512]{2,1,0:T(8,128)S(1)}, f32[1,16,512]{2,1,0:T(8,128)S(1)}, u32[]{:S(2)}, u32[]{:S(2)}) collective-permute-start(f32[1,16,512]{2,1,0:T(8,128)S(1)} %get-tuple-element.6), channel_id=1, source_target_pairs={{0,256},{32,288},{64,320},{96,352},{128,384},{160,416},{192,448},{... | collective-permute-start | bytes 98312 | tf_op jit(solution)/shard_map/ppermute | solution.py:33
  159.3 7.5 %collective-permute-start.4 = (f32[1,16,512]{2,1,0:T(8,128)S(1)}, f32[1,16,512]{2,1,0:T(8,128)S(1)}, u32[]{:S(2)}, u32[]{:S(2)}) collective-permute-start(f32[1,16,512]{2,1,0:T(8,128)S(1)} %get-tuple-element.5), channel_id=1, source_target_pairs={{0,384},{32,416},{64,448},{96,480},{128,256},{160,288},{192,320},{... | collective-permute-start | bytes 98312 | tf_op jit(solution)/shard_map/ppermute | solution.py:33

commit v4 on v3

--- a/solution.py
+++ b/solution.py
@@ -19,20 +19,15 @@
     return lax.all_to_all(chunks, axis, 0, 0)
 
 
-def fold(chunks, axis):
-    me = lax.axis_index(axis).astype(jnp.uint32)
-    n, shift = chunks.shape[0], 0
-    while n > 1:
-        radix = n if n <= 4 else 2
-        groups = chunks.reshape((n // radix, radix) + chunks.shape[1:])
-        digit = (me >> shift) & (radix - 1)
-        chunks = lax.dynamic_index_in_dim(groups, digit, 1, keepdims=False)
-        for d in range(1, radix):
-            sent = lax.dynamic_index_in_dim(groups, digit ^ d, 1, keepdims=False)
-            partner = [(k, k ^ (d << shift)) for k in range(lax.axis_size(axis))]
-            chunks = chunks + lax.ppermute(sent, axis, partner)
-        n, shift = n // radix, shift + radix.bit_length() - 1
-    return chunks[0]
+def fold(groups, dim, axis, shift):
+    size = groups.shape[dim]
+    digit = (lax.axis_index(axis).astype(jnp.uint32) >> shift) & (size - 1)
+    total = lax.dynamic_index_in_dim(groups, digit, dim, keepdims=False)
+    for d in range(1, size):
+        sent = lax.dynamic_index_in_dim(groups, digit ^ d, dim, keepdims=False)
+        partner = [(k, k ^ (d << shift)) for k in range(lax.axis_size(axis))]
+        total = total + lax.ppermute(sent, axis, partner)
+    return total
 
 
 def lse(values, dim):
@@ -77,10 +72,13 @@
         col_pot = log_weight - shared_lse(lse(row_pot[:, None] + score, 0), "row")
     plan = jnp.exp(row_pot[:, None] + col_pot[None, :] + score)
     factor = -batch * scale
+    conf_term = matmul(graph_t, plan, ((1,), (0,)), lax.Precision.HIGH) * factor
+    digits = conf_term.reshape(lax.axis_size("row") // 4, 2, 2, -1, cols)
+    digits = fold(digits, 1, "row", 1)
     graph_term = matmul(conf_t, plan, ((1,), (1,)), lax.Precision.HIGH) * factor
     graph_parts = swap(graph_term.reshape(lax.axis_size("col"), -1, rows), "col")
-    conf_term = matmul(graph_t, plan, ((1,), (0,)), lax.Precision.HIGH) * factor
-    grad_conf = fold(conf_term.reshape(lax.axis_size("row"), -1, cols), "row").T
+    digits = fold(digits, 1, "row", 0)
+    grad_conf = fold(digits, 0, "row", 2).T
     grad_graph = jnp.sum(graph_parts, axis=0).T
     return (grad_graph, grad_conf, row_pot, col_pot)
 

time: 170 us -> 172 us (1.012)
  waiting for transfers between devices: 7.88 us -> 9.81 us
    ppermute x5, waiting for transfers between devices: 7.88 us -> 9.8 us  [fold(): total = total + lax.ppermute(sent, axis, partner)]
  transfers between devices with their start and end apart: 7 -> 7, of which waited for: 3 -> 3; matrix products, arithmetic and copies ran while one was open for 3% -> 2% of each run, Pallas kernels for 0% -> 0%
where the time goes in v4:
time: 172 us; the launch traced here: 171 us
  blocking collectives  111 us (65%)
  starting transfers between devices  31.2 us (18%)
  waiting for transfers between devices  9.81 us (6%)
  matrix products  8.04 us (5%)
  other arithmetic  7.07 us (4%)
  local copies, waits for them, and re-layouts  2.8 us (2%)
    all_to_all x6, blocking collectives, spread(): lax.all_to_all(jnp.broadcast_to(block[None], (n,) + block.shape), axis, 0...  85.6 us
    all_gather x1, blocking collectives, gather_parts(): conf_t = lax.all_gather(conf_part, 'row')  25.4 us
    ppermute x5, starting transfers between devices, fold(): total = total + lax.ppermute(sent, axis, partner)  16.7 us
    all_to_all x1, starting transfers between devices, spread(): lax.all_to_all(jnp.broadcast_to(block[None], (n,) + block.shape), axis, 0...  10.6 us
    ppermute x5, waiting for transfers between devices, fold(): total = total + lax.ppermute(sent, axis, partner)  9.8 us
    dot_general x3, matrix products, matmul(): lax.dot_general(lhs, rhs, (contract, ((), ())), precision=precision, pref...  8.04 us
    all_to_all x1, starting transfers between devices, swap(): return lax.all_to_all(chunks, axis, 0, 0)  3.93 us
  transfers between devices with their start and end apart: 7, of which 3 were waited for; matrix products, arithmetic and copies ran while one was open for 2% of the time, Pallas kernels for 0%

profile of v4, /device:TPU:1, one launch (start us, length us, event | category | flops | bytes accessed | tf_op | source)
XLA Modules:
  0.0 170.9 jit_solution(10291847735349158618)
XLA Ops:
  0.6 1.9 %broadcast_in_dim.14 = f32[32,8,1024]{2,1,0:T(8,128)} broadcast(f32[8,1024]{1,0:T(8,128)} %bitcast.69), dimensions={1,2} | broadcast | bytes 1081344 | tf_op jit(solution)/shard_map/broadcast_in_dim | solution.py:15
  2.5 10.6 %all-to-all-start = ((f32[32,8,1024]{2,1,0:T(8,128)}), f32[32,8,1024]{2,1,0:T(8,128)}, u32[]{:S(2)}, u32[]{:S(2)}) async-start(f32[32,8,1024]{2,1,0:T(8,128)} %broadcast_in_dim.14), calls=%async_computation | async-start | bytes 2097152 | tf_op jit(solution)/shard_map/all_to_all | solution.py:15
  13.1 25.4 %all-gather = f32[256,512]{1,0:T(8,128)S(1)} all-gather(f32[16,512]{1,0:T(8,128)S(1)} %bitcast.70), channel_id=2, replica_groups=mesh['row'=16,'col'=32] {'row'}, dimensions={0}, use_global_device_ids=true | all-gather | bytes 557056 | tf_op jit(solution)/shard_map/all_gather | solution.py:46
  38.5 3.2 %fusion.14 = (f32[1024]{0:T(1024)S(1)}, f32[1024,512]{1,0:T(8,128)S(1)}) fusion(f32[256,512]{1,0:T(8,128)S(1)} %all-gather, f32[32,8,1024]{2,1,0:T(8,128)} %all-to-all-done), kind=kOutput, calls=%fused_computation.53 | convolution fusion | flops 1611660288 | bytes 3674112 | tf_op jit(solution)/shard_map/dot_general | solution.py:51
  41.7 0.7 exponential_reduce_fusion.5
  42.5 18.4 %all_to_all.40 = f32[32,8,128]{2,1,0:T(8,128)S(1)} all-to-all(f32[32,8,128]{2,1,0:T(8,128)S(1)} %broadcast_in_dim.15), channel_id=1, replica_groups=mesh['row'=16,'col'=32] {'col'}, dimensions={0} | all-to-all | bytes 262144 | tf_op jit(solution)/shard_map/all_to_all | solution.py:15
  61.2 0.4 exponential_reduce_fusion.4
  61.6 18.6 %all_to_all.41 = f32[16,4,128]{2,1,0:T(4,128)S(1)} all-to-all(f32[16,4,128]{2,1,0:T(4,128)S(1)} %broadcast_in_dim.16), channel_id=1, replica_groups=mesh['row'=16,'col'=32] {'row'}, dimensions={0} | all-to-all | bytes 65536 | tf_op jit(solution)/shard_map/all_to_all | solution.py:15
  80.5 0.6 exponential_reduce_fusion.3
  81.1 12.3 %all_to_all.42 = f32[32,8,128]{2,1,0:T(8,128)S(1)} all-to-all(f32[32,8,128]{2,1,0:T(8,128)S(1)} %broadcast_in_dim.17), channel_id=1, replica_groups=mesh['row'=16,'col'=32] {'col'}, dimensions={0} | all-to-all | bytes 262144 | tf_op jit(solution)/shard_map/all_to_all | solution.py:15
  93.5 0.2 add_reduce_fusion.2
  93.7 0.4 exponential_reduce_fusion.2
  94.2 12.0 %all_to_all.43 = f32[16,4,128]{2,1,0:T(4,128)S(1)} all-to-all(f32[16,4,128]{2,1,0:T(4,128)S(1)} %broadcast_in_dim.18), channel_id=1, replica_groups=mesh['row'=16,'col'=32] {'row'}, dimensions={0} | all-to-all | bytes 65536 | tf_op jit(solution)/shard_map/all_to_all | solution.py:15
  106.5 0.6 exponential_reduce_fusion.1
  107.1 12.4 %all_to_all.44 = f32[32,8,128]{2,1,0:T(8,128)S(1)} all-to-all(f32[32,8,128]{2,1,0:T(8,128)S(1)} %broadcast_in_dim.19), channel_id=1, replica_groups=mesh['row'=16,'col'=32] {'col'}, dimensions={0} | all-to-all | bytes 262144 | tf_op jit(solution)/shard_map/all_to_all | solution.py:15
  119.8 0.4 exponential_reduce_fusion
  120.3 12.0 %all_to_all.45 = f32[16,4,128]{2,1,0:T(4,128)S(1)} all-to-all(f32[16,4,128]{2,1,0:T(4,128)S(1)} %broadcast_in_dim.20), channel_id=1, replica_groups=mesh['row'=16,'col'=32] {'row'}, dimensions={0} | all-to-all | bytes 65536 | tf_op jit(solution)/shard_map/all_to_all | solution.py:15
  132.3 2.3 %fusion.3 = f32[32,8,1024]{2,1,0:T(8,128)} fusion(f32[256,512]{1,0:T(8,128)S(1)} %all-gather, f32[1024,512]{1,0:T(8,128)S(1)} %get-tuple-element.8, f32[512]{0:T(512)S(1)} %subtract_bitcast_fusion.3, f32[1024]{0:T(1024)S(1)} %subtract_bitcast_fusion), kind=kOutput, calls=%fused_computation.16 | convolution fusion | flops 806617088 | bytes 3676160 | tf_op jit(solution)/shard_map/dot_general | solution.py:51
  134.6 3.9 %all-to-all-start.7 = ((f32[32,8,1024]{2,1,0:T(8,128)}), f32[32,8,1024]{2,1,0:T(8,128)S(1)}, u32[]{:S(2)}, u32[]{:S(2)}) async-start(f32[32,8,1024]{2,1,0:T(8,128)} %fusion.3), calls=%async_computation.7 | async-start | bytes 2097152 | tf_op jit(solution)/shard_map/all_to_all | solution.py:19
  138.6 2.6 %fusion.4 = f32[512,256]{0,1:T(8,128)S(1)} fusion(f32[1024,512]{1,0:T(8,128)S(1)} %get-tuple-element.8, f32[32,8,1024]{2,1,0:T(8,128)} %all-to-all-done, f32[512]{0:T(512)S(1)} %subtract_bitcast_fusion.3, f32[1024]{0:T(1024)S(1)} %subtract_bitcast_fusion), kind=kOutput, calls=%fused_computation.17 | convolution fusion | flops 806486016 | bytes 3676160 | tf_op jit(solution)/shard_map/dot_general | solution.py:51
  141.2 0.8 copy-done
  142.0 2.1 %collective-permute-start = (f32[4,2,16,512]{3,2,1,0:T(8,128)S(1)}, f32[4,2,16,512]{3,2,1,0:T(8,128)S(1)}, u32[]{:S(2)}, u32[]{:S(2)}) collective-permute-start(f32[4,2,16,512]{3,2,1,0:T(8,128)S(1)} %dynamic-slice_bitcast_fusion), channel_id=1, source_target_pairs={{0,64},{32,96},{64,0},{96,32},{128,192},{160,224},{192,128},{224,1... | collective-permute-start | bytes 786440 | tf_op jit(solution)/shard_map/ppermute | solution.py:29
  144.1 7.2 %collective-permute-done = f32[4,2,16,512]{3,2,1,0:T(8,128)S(1)} collective-permute-done((f32[4,2,16,512]{3,2,1,0:T(8,128)S(1)}, f32[4,2,16,512]{3,2,1,0:T(8,128)S(1)}, u32[]{:S(2)}, u32[]{:S(2)}) %collective-permute-start) | collective-permute-done | bytes 262176 | tf_op jit(solution)/shard_map/ppermute | solution.py:29
  151.4 1.0 bitcast_add_fusion
  152.4 3.2 %collective-permute-start.1 = (f32[4,16,512]{2,1,0:T(8,128)S(1)}, f32[4,16,512]{2,1,0:T(8,128)S(1)}, u32[]{:S(2)}, u32[]{:S(2)}) collective-permute-start(f32[4,16,512]{2,1,0:T(8,128)S(1)} %dynamic-slice_bitcast_fusion.1), channel_id=1, source_target_pairs={{0,32},{32,0},{64,96},{96,64},{128,160},{160,128},{192,224},{224,1... | collective-permute-start | bytes 393224 | tf_op jit(solution)/shard_map/ppermute | solution.py:29
  155.5 1.0 collective-permute-done.1
  156.5 2.2 %collective-permute-start.2 = (f32[16,512]{1,0:T(8,128)S(1)}, f32[16,512]{1,0:T(8,128)S(1)}, u32[]{:S(2)}, u32[]{:S(2)}) collective-permute-start(f32[16,512]{1,0:T(8,128)S(1)} %get-tuple-element.4), channel_id=1, source_target_pairs={{0,128},{32,160},{64,192},{96,224},{128,0},{160,32},{192,64},{224,... | collective-permute-start | bytes 98312 | tf_op jit(solution)/shard_map/ppermute | solution.py:29
  158.8 3.9 %collective-permute-start.3 = (f32[16,512]{1,0:T(8,128)S(1)}, f32[16,512]{1,0:T(8,128)S(1)}, u32[]{:S(2)}, u32[]{:S(2)}) collective-permute-start(f32[16,512]{1,0:T(8,128)S(1)} %get-tuple-element.6), channel_id=1, source_target_pairs={{0,256},{32,288},{64,320},{96,352},{128,384},{160,416},{192,448},{... | collective-permute-start | bytes 98312 | tf_op jit(solution)/shard_map/ppermute | solution.py:29
  162.7 5.2 %collective-permute-start.4 = (f32[16,512]{1,0:T(8,128)S(1)}, f32[16,512]{1,0:T(8,128)S(1)}, u32[]{:S(2)}, u32[]{:S(2)}) collective-permute-start(f32[16,512]{1,0:T(8,128)S(1)} %get-tuple-element.5), channel_id=1, source_target_pairs={{0,384},{32,416},{64,448},{96,480},{128,256},{160,288},{192,320},{... | collective-permute-start | bytes 98312 | tf_op jit(solution)/shard_map/ppermute | solution.py:29
  168.0 1.6 collective-permute-done.4
  169.6 0.6 fusion.13
  170.2 0.7 reduce_sum.129
  (49 shorter events, 1.6 us)
Async XLA Ops:
  0.6 12.5 %copy-start.2 = (f32[512,16]{0,1:T(8,128)S(1)}, f32[512,16]{0,1:T(8,128)}, u32[]{:S(2)}) copy-start(f32[512,16]{0,1:T(8,128)} %param.3) | copy-start | bytes 98308
  2.5 36.0 %all-to-all-start = ((f32[32,8,1024]{2,1,0:T(8,128)}), f32[32,8,1024]{2,1,0:T(8,128)}, u32[]{:S(2)}, u32[]{:S(2)}) async-start(f32[32,8,1024]{2,1,0:T(8,128)} %broadcast_in_dim.14), calls=%async_computation | async-start | bytes 2097152 | tf_op jit(solution)/shard_map/all_to_all | solution.py:15
  119.6 19.0 %copy-start.1 = (f32[1024]{0:T(1024)}, f32[1024]{0:T(1024)S(1)}, u32[]{:S(2)}) copy-start(f32[1024]{0:T(1024)S(1)} %subtract_bitcast_fusion) | copy-start | bytes 12292
  132.3 6.3 %copy-start.3 = (f32[512]{0:T(512)}, f32[512]{0:T(512)S(1)}, u32[]{:S(2)}) copy-start(f32[512]{0:T(512)S(1)} %subtract_bitcast_fusion.3) | copy-start | bytes 6148
  134.6 35.6 %all-to-all-start.7 = ((f32[32,8,1024]{2,1,0:T(8,128)}), f32[32,8,1024]{2,1,0:T(8,128)S(1)}, u32[]{:S(2)}, u32[]{:S(2)}) async-start(f32[32,8,1024]{2,1,0:T(8,128)} %fusion.3), calls=%async_computation.7 | async-start | bytes 2097152 | tf_op jit(solution)/shard_map/all_to_all | solution.py:19
  141.1 0.8 copy-start
  142.0 9.4 %collective-permute-start = (f32[4,2,16,512]{3,2,1,0:T(8,128)S(1)}, f32[4,2,16,512]{3,2,1,0:T(8,128)S(1)}, u32[]{:S(2)}, u32[]{:S(2)}) collective-permute-start(f32[4,2,16,512]{3,2,1,0:T(8,128)S(1)} %dynamic-slice_bitcast_fusion), channel_id=1, source_target_pairs={{0,64},{32,96},{64,0},{96,32},{128,192},{160,224},{192,128},{224,1... | collective-permute-start | bytes 786440 | tf_op jit(solution)/shard_map/ppermute | solution.py:29
  152.4 4.1 %collective-permute-start.1 = (f32[4,16,512]{2,1,0:T(8,128)S(1)}, f32[4,16,512]{2,1,0:T(8,128)S(1)}, u32[]{:S(2)}, u32[]{:S(2)}) collective-permute-start(f32[4,16,512]{2,1,0:T(8,128)S(1)} %dynamic-slice_bitcast_fusion.1), channel_id=1, source_target_pairs={{0,32},{32,0},{64,96},{96,64},{128,160},{160,128},{192,224},{224,1... | collective-permute-start | bytes 393224 | tf_op jit(solution)/shard_map/ppermute | solution.py:29
  156.5 11.4 %collective-permute-start.2 = (f32[16,512]{1,0:T(8,128)S(1)}, f32[16,512]{1,0:T(8,128)S(1)}, u32[]{:S(2)}, u32[]{:S(2)}) collective-permute-start(f32[16,512]{1,0:T(8,128)S(1)} %get-tuple-element.4), channel_id=1, source_target_pairs={{0,128},{32,160},{64,192},{96,224},{128,0},{160,32},{192,64},{224,... | collective-permute-start | bytes 98312 | tf_op jit(solution)/shard_map/ppermute | solution.py:29
  158.8 9.2 %collective-permute-start.3 = (f32[16,512]{1,0:T(8,128)S(1)}, f32[16,512]{1,0:T(8,128)S(1)}, u32[]{:S(2)}, u32[]{:S(2)}) collective-permute-start(f32[16,512]{1,0:T(8,128)S(1)} %get-tuple-element.6), channel_id=1, source_target_pairs={{0,256},{32,288},{64,320},{96,352},{128,384},{160,416},{192,448},{... | collective-permute-start | bytes 98312 | tf_op jit(solution)/shard_map/ppermute | solution.py:29
  162.7 6.9 %collective-permute-start.4 = (f32[16,512]{1,0:T(8,128)S(1)}, f32[16,512]{1,0:T(8,128)S(1)}, u32[]{:S(2)}, u32[]{:S(2)}) collective-permute-start(f32[16,512]{1,0:T(8,128)S(1)} %get-tuple-element.5), channel_id=1, source_target_pairs={{0,384},{32,416},{64,448},{96,480},{128,256},{160,288},{192,320},{... | collective-permute-start | bytes 98312 | tf_op jit(solution)/shard_map/ppermute | solution.py:29

commit v5 on v3

--- a/solution.py
+++ b/solution.py
@@ -35,15 +35,16 @@
     return chunks[0]
 
 
-def lse(values, dim):
+def local_lse(values, dim):
     peak = jnp.max(values, axis=dim, keepdims=True)
-    total = jnp.sum(jnp.exp(values - peak), axis=dim)
-    return jnp.squeeze(peak, dim) + jnp.log(total)
+    mass = jnp.exp(values - peak)
+    peak = jnp.squeeze(peak, dim)
+    return peak + jnp.log(jnp.sum(mass, axis=dim)), peak, mass
 
 
 def shared_lse(partial, axis):
     parts = spread(partial.reshape(-1, LANES), axis)
-    return lse(parts, 0).reshape(partial.shape)
+    return local_lse(parts, 0)[0].reshape(partial.shape)
 
 
 def gather_parts(graph_part, conf_part):
@@ -73,13 +74,18 @@
     row_pot = jnp.zeros((rows,), jnp.float32)
     col_pot = jnp.zeros((cols,), jnp.float32)
     for _ in range(ITERS):
-        row_pot = log_weight - shared_lse(lse(col_pot[None, :] + score, 1), "col")
-        col_pot = log_weight - shared_lse(lse(row_pot[:, None] + score, 0), "row")
+        partial, _, _ = local_lse(col_pot[None, :] + score, 1)
+        row_pot = log_weight - shared_lse(partial, "col")
+        partial, col_peak, mass = local_lse(row_pot[:, None] + score, 0)
+        col_pot = log_weight - shared_lse(partial, "row")
+    factor = -batch * scale
+    conf_mass = matmul(graph_t, mass, ((1,), (0,)), lax.Precision.HIGH)
+    conf_mass = lax.optimization_barrier(conf_mass)
+    col_scale = factor * jnp.exp(col_peak + col_pot)
     plan = jnp.exp(row_pot[:, None] + col_pot[None, :] + score)
-    factor = -batch * scale
     graph_term = matmul(conf_t, plan, ((1,), (1,)), lax.Precision.HIGH) * factor
     graph_parts = swap(graph_term.reshape(lax.axis_size("col"), -1, rows), "col")
-    conf_term = matmul(graph_t, plan, ((1,), (0,)), lax.Precision.HIGH) * factor
+    conf_term = conf_mass * col_scale
     grad_conf = fold(conf_term.reshape(lax.axis_size("row"), -1, cols), "row").T
     grad_graph = jnp.sum(graph_parts, axis=0).T
     return (grad_graph, grad_conf, row_pot, col_pot)

time: 170 us -> 171 us (level)
  blocking collectives: 111 us -> 99.1 us
  waiting for transfers between devices: 7.88 us -> 15.4 us
  starting transfers between devices: 30.4 us -> 35.9 us
    all_to_all x6 -> x5, blocking collectives: 85.6 us -> 73.7 us  [spread(): lax.all_to_all(jnp.broadcast_to(block[None], (n,) + block.shape), axis, 0...]
    all_to_all x1 -> x2, waiting for transfers between devices: 0.01 us -> 7.48 us  [spread(): lax.all_to_all(jnp.broadcast_to(block[None], (n,) + block.shape), axis, 0...]
    all_to_all x1 -> x2, starting transfers between devices: 10.6 us -> 16 us  [spread(): lax.all_to_all(jnp.broadcast_to(block[None], (n,) + block.shape), axis, 0...]
  transfers between devices with their start and end apart: 7 -> 8, of which waited for: 3 -> 4; matrix products, arithmetic and copies ran while one was open for 3% -> 3% of each run, Pallas kernels for 0% -> 0%
where the time goes in v5:
time: 171 us; the launch traced here: 169 us
  blocking collectives  99.1 us (58%)
  starting transfers between devices  35.9 us (21%)
  waiting for transfers between devices  15.4 us (9%)
  matrix products  8.72 us (5%)
  other arithmetic  6.25 us (4%)
  local copies, waits for them, and re-layouts  2.85 us (2%)
    all_to_all x5, blocking collectives, spread(): lax.all_to_all(jnp.broadcast_to(block[None], (n,) + block.shape), axis, 0...  73.7 us
    all_gather x1, blocking collectives, gather_parts(): conf_t = lax.all_gather(conf_part, 'row')  25.4 us
    all_to_all x2, starting transfers between devices, spread(): lax.all_to_all(jnp.broadcast_to(block[None], (n,) + block.shape), axis, 0...  16 us
    ppermute x5, starting transfers between devices, fold(): chunks = chunks + lax.ppermute(sent, axis, partner)  15.8 us
    dot_general x3, matrix products, matmul(): lax.dot_general(lhs, rhs, (contract, ((), ())), precision=precision, pref...  8.72 us
    ppermute x5, waiting for transfers between devices, fold(): chunks = chunks + lax.ppermute(sent, axis, partner)  7.87 us
    all_to_all x2, waiting for transfers between devices, spread(): lax.all_to_all(jnp.broadcast_to(block[None], (n,) + block.shape), axis, 0...  7.48 us
    all_to_all x1, starting transfers between devices, swap(): return lax.all_to_all(chunks, axis, 0, 0)  4.11 us
  transfers between devices with their start and end apart: 8, of which 4 were waited for; matrix products, arithmetic and copies ran while one was open for 3% of the time, Pallas kernels for 0%

profile of v5, /device:TPU:1, one launch (start us, length us, event | category | flops | bytes accessed | tf_op | source)
XLA Modules:
  0.0 169.1 jit_solution(3453147462201231456)
XLA Ops:
  0.6 1.9 %broadcast_in_dim.14 = f32[32,8,1024]{2,1,0:T(8,128)} broadcast(f32[8,1024]{1,0:T(8,128)} %bitcast.61), dimensions={1,2} | broadcast | bytes 1081344 | tf_op jit(solution)/shard_map/broadcast_in_dim | solution.py:15
  2.6 10.6 %all-to-all-start = ((f32[32,8,1024]{2,1,0:T(8,128)}), f32[32,8,1024]{2,1,0:T(8,128)}, u32[]{:S(2)}, u32[]{:S(2)}) async-start(f32[32,8,1024]{2,1,0:T(8,128)} %broadcast_in_dim.14), calls=%async_computation | async-start | bytes 2097152 | tf_op jit(solution)/shard_map/all_to_all | solution.py:15
  13.2 25.4 %all-gather = f32[256,512]{1,0:T(8,128)S(1)} all-gather(f32[16,512]{1,0:T(8,128)S(1)} %bitcast.62), channel_id=2, replica_groups=mesh['row'=16,'col'=32] {'row'}, dimensions={0}, use_global_device_ids=true | all-gather | bytes 557056 | tf_op jit(solution)/shard_map/all_gather | solution.py:52
  38.6 3.2 %fusion.19 = (f32[1024]{0:T(1024)S(1)}, f32[1024,512]{1,0:T(8,128)S(1)}) fusion(f32[256,512]{1,0:T(8,128)S(1)} %all-gather, f32[32,8,1024]{2,1,0:T(8,128)} %all-to-all-done), kind=kOutput, calls=%fused_computation.55 | convolution fusion | flops 1611660288 | bytes 3674112 | tf_op jit(solution)/shard_map/dot_general | solution.py:57
  41.8 0.7 exponential_reduce_fusion.4
  42.5 18.4 %all_to_all.40 = f32[32,8,128]{2,1,0:T(8,128)S(1)} all-to-all(f32[32,8,128]{2,1,0:T(8,128)S(1)} %broadcast_in_dim.15), channel_id=1, replica_groups=mesh['row'=16,'col'=32] {'col'}, dimensions={0} | all-to-all | bytes 262144 | tf_op jit(solution)/shard_map/all_to_all | solution.py:15
  61.2 0.4 exponential_reduce_fusion.3
  61.7 18.6 %all_to_all.41 = f32[16,4,128]{2,1,0:T(4,128)S(1)} all-to-all(f32[16,4,128]{2,1,0:T(4,128)S(1)} %broadcast_in_dim.16), channel_id=1, replica_groups=mesh['row'=16,'col'=32] {'row'}, dimensions={0} | all-to-all | bytes 65536 | tf_op jit(solution)/shard_map/all_to_all | solution.py:15
  80.5 0.6 exponential_reduce_fusion.2
  81.1 12.3 %all_to_all.42 = f32[32,8,128]{2,1,0:T(8,128)S(1)} all-to-all(f32[32,8,128]{2,1,0:T(8,128)S(1)} %broadcast_in_dim.17), channel_id=1, replica_groups=mesh['row'=16,'col'=32] {'col'}, dimensions={0} | all-to-all | bytes 262144 | tf_op jit(solution)/shard_map/all_to_all | solution.py:15
  93.5 0.2 add_reduce_fusion.2
  93.8 0.4 exponential_reduce_fusion.1
  94.2 12.0 %all_to_all.43 = f32[16,4,128]{2,1,0:T(4,128)S(1)} all-to-all(f32[16,4,128]{2,1,0:T(4,128)S(1)} %broadcast_in_dim.18), channel_id=1, replica_groups=mesh['row'=16,'col'=32] {'row'}, dimensions={0} | all-to-all | bytes 65536 | tf_op jit(solution)/shard_map/all_to_all | solution.py:15
  106.5 0.6 exponential_reduce_fusion
  107.1 12.4 %all_to_all.44 = f32[32,8,128]{2,1,0:T(8,128)S(1)} all-to-all(f32[32,8,128]{2,1,0:T(8,128)S(1)} %broadcast_in_dim.19), channel_id=1, replica_groups=mesh['row'=16,'col'=32] {'col'}, dimensions={0} | all-to-all | bytes 262144 | tf_op jit(solution)/shard_map/all_to_all | solution.py:15
  119.8 0.4 fusion.5
  120.3 0.6 broadcast_in_dim.20
  120.9 5.4 %all-to-all-start.6 = ((f32[16,4,128]{2,1,0:T(4,128)}), f32[16,4,128]{2,1,0:T(4,128)S(1)}, u32[]{:S(2)}, u32[]{:S(2)}) async-start(f32[16,4,128]{2,1,0:T(4,128)} %broadcast_in_dim.20), calls=%async_computation.6 | async-start | bytes 65536 | tf_op jit(solution)/shard_map/all_to_all | solution.py:15
  126.3 7.5 %all-to-all-done.6 = f32[16,4,128]{2,1,0:T(4,128)S(1)} async-done(((f32[16,4,128]{2,1,0:T(4,128)}), f32[16,4,128]{2,1,0:T(4,128)S(1)}, u32[]{:S(2)}, u32[]{:S(2)}) %all-to-all-start.6) | async-done | bytes 32800 | tf_op jit(solution)/shard_map/all_to_all | solution.py:15
  133.9 2.3 %fusion.9 = f32[32,8,1024]{2,1,0:T(8,128)} fusion(f32[256,512]{1,0:T(8,128)S(1)} %all-gather, f32[1024,512]{1,0:T(8,128)S(1)} %get-tuple-element.10, f32[512]{0:T(512)S(1)} %get-tuple-element.5, f32[1024]{0:T(1024)S(1)} %subtract_bitcast_fusion), kind=kOutput, calls=%fused_computation.19 | convolution fusion | flops 806617088 | bytes 3676160 | tf_op jit(solution)/shard_map/dot_general | solution.py:57
  136.2 4.1 %all-to-all-start.7 = ((f32[32,8,1024]{2,1,0:T(8,128)}), f32[32,8,1024]{2,1,0:T(8,128)S(1)}, u32[]{:S(2)}, u32[]{:S(2)}) async-start(f32[32,8,1024]{2,1,0:T(8,128)} %fusion.9), calls=%async_computation.7 | async-start | bytes 2097152 | tf_op jit(solution)/shard_map/all_to_all | solution.py:19
  140.3 3.2 %fusion.12 = f32[256,512]{0,1:T(8,128)S(1)} fusion(f32[1024,512]{1,0:T(8,128)S(1)} %get-tuple-element.10, f32[32,8,1024]{2,1,0:T(8,128)} %all-to-all-done, f32[512]{0:T(512)S(1)} %add_reduce_fusion, f32[1024]{0:T(1024)S(1)} %subtract_bitcast_fusion), kind=kOutput, calls=%fused_computation.20 | convolution fusion | flops 806354944 | bytes 3676160 | tf_op jit(solution)/shard_map/dot_general | solution.py:57
  143.9 2.3 %collective-permute-start = (f32[8,16,512]{2,1,0:T(8,128)S(1)}, f32[8,16,512]{2,1,0:T(8,128)S(1)}, u32[]{:S(2)}, u32[]{:S(2)}) collective-permute-start(f32[8,16,512]{2,1,0:T(8,128)S(1)} %dynamic-slice_bitcast_fusion), channel_id=1, source_target_pairs={{0,32},{32,0},{64,96},{96,64},{128,160},{160,128},{192,224},{224,1... | collective-permute-start | bytes 786440 | tf_op jit(solution)/shard_map/ppermute | solution.py:33
  146.3 1.1 collective-permute-done
  147.5 2.1 %collective-permute-start.1 = (f32[4,16,512]{2,1,0:T(8,128)S(1)}, f32[4,16,512]{2,1,0:T(8,128)S(1)}, u32[]{:S(2)}, u32[]{:S(2)}) collective-permute-start(f32[4,16,512]{2,1,0:T(8,128)S(1)} %dynamic-slice_bitcast_fusion.1), channel_id=1, source_target_pairs={{0,64},{32,96},{64,0},{96,32},{128,192},{160,224},{192,128},{224,1... | collective-permute-start | bytes 393224 | tf_op jit(solution)/shard_map/ppermute | solution.py:33
  149.6 4.4 %collective-permute-done.1 = f32[4,16,512]{2,1,0:T(8,128)S(1)} collective-permute-done((f32[4,16,512]{2,1,0:T(8,128)S(1)}, f32[4,16,512]{2,1,0:T(8,128)S(1)}, u32[]{:S(2)}, u32[]{:S(2)}) %collective-permute-start.1) | collective-permute-done | bytes 131104 | tf_op jit(solution)/shard_map/ppermute | solution.py:33
  154.1 2.2 %collective-permute-start.2 = (f32[1,16,512]{2,1,0:T(8,128)S(1)}, f32[1,16,512]{2,1,0:T(8,128)S(1)}, u32[]{:S(2)}, u32[]{:S(2)}) collective-permute-start(f32[1,16,512]{2,1,0:T(8,128)S(1)} %get-tuple-element.6), channel_id=1, source_target_pairs={{0,128},{32,160},{64,192},{96,224},{128,0},{160,32},{192,64},{224,... | collective-permute-start | bytes 98312 | tf_op jit(solution)/shard_map/ppermute | solution.py:33
  156.3 3.9 %collective-permute-start.3 = (f32[1,16,512]{2,1,0:T(8,128)S(1)}, f32[1,16,512]{2,1,0:T(8,128)S(1)}, u32[]{:S(2)}, u32[]{:S(2)}) collective-permute-start(f32[1,16,512]{2,1,0:T(8,128)S(1)} %get-tuple-element.8), channel_id=1, source_target_pairs={{0,256},{32,288},{64,320},{96,352},{128,384},{160,416},{192,448},{... | collective-permute-start | bytes 98312 | tf_op jit(solution)/shard_map/ppermute | solution.py:33
  160.3 5.2 %collective-permute-start.4 = (f32[1,16,512]{2,1,0:T(8,128)S(1)}, f32[1,16,512]{2,1,0:T(8,128)S(1)}, u32[]{:S(2)}, u32[]{:S(2)}) collective-permute-start(f32[1,16,512]{2,1,0:T(8,128)S(1)} %get-tuple-element.7), channel_id=1, source_target_pairs={{0,384},{32,416},{64,448},{96,480},{128,256},{160,288},{192,320},{... | collective-permute-start | bytes 98312 | tf_op jit(solution)/shard_map/ppermute | solution.py:33
  165.5 2.3 %collective-permute-done.4 = f32[1,16,512]{2,1,0:T(8,128)S(1)} collective-permute-done((f32[1,16,512]{2,1,0:T(8,128)S(1)}, f32[1,16,512]{2,1,0:T(8,128)S(1)}, u32[]{:S(2)}, u32[]{:S(2)}) %collective-permute-start.4) | collective-permute-done | bytes 32800 | tf_op jit(solution)/shard_map/ppermute | solution.py:33
  167.8 0.6 add_bitcast_fusion
  168.4 0.7 reduce_sum.129
  (50 shorter events, 2.0 us)
Async XLA Ops:
  0.6 12.6 %copy-start.1 = (f32[512,16]{0,1:T(8,128)S(1)}, f32[512,16]{0,1:T(8,128)}, u32[]{:S(2)}) copy-start(f32[512,16]{0,1:T(8,128)} %param.3) | copy-start | bytes 98308
  2.6 36.0 %all-to-all-start = ((f32[32,8,1024]{2,1,0:T(8,128)}), f32[32,8,1024]{2,1,0:T(8,128)}, u32[]{:S(2)}, u32[]{:S(2)}) async-start(f32[32,8,1024]{2,1,0:T(8,128)} %broadcast_in_dim.14), calls=%async_computation | async-start | bytes 2097152 | tf_op jit(solution)/shard_map/all_to_all | solution.py:15
  119.6 20.7 %copy-start = (f32[1024]{0:T(1024)}, f32[1024]{0:T(1024)S(1)}, u32[]{:S(2)}) copy-start(f32[1024]{0:T(1024)S(1)} %subtract_bitcast_fusion) | copy-start | bytes 12292
  120.9 12.9 %all-to-all-start.6 = ((f32[16,4,128]{2,1,0:T(4,128)}), f32[16,4,128]{2,1,0:T(4,128)S(1)}, u32[]{:S(2)}, u32[]{:S(2)}) async-start(f32[16,4,128]{2,1,0:T(4,128)} %broadcast_in_dim.20), calls=%async_computation.6 | async-start | bytes 65536 | tf_op jit(solution)/shard_map/all_to_all | solution.py:15
  133.9 2.3 %copy-start.2 = (f32[512]{0:T(512)}, f32[512]{0:T(512)S(1)}, u32[]{:S(2)}) copy-start(f32[512]{0:T(512)S(1)} %get-tuple-element.5) | copy-start | bytes 6148
  136.2 32.2 %all-to-all-start.7 = ((f32[32,8,1024]{2,1,0:T(8,128)}), f32[32,8,1024]{2,1,0:T(8,128)S(1)}, u32[]{:S(2)}, u32[]{:S(2)}) async-start(f32[32,8,1024]{2,1,0:T(8,128)} %fusion.9), calls=%async_computation.7 | async-start | bytes 2097152 | tf_op jit(solution)/shard_map/all_to_all | solution.py:19
  143.9 3.5 %collective-permute-start = (f32[8,16,512]{2,1,0:T(8,128)S(1)}, f32[8,16,512]{2,1,0:T(8,128)S(1)}, u32[]{:S(2)}, u32[]{:S(2)}) collective-permute-start(f32[8,16,512]{2,1,0:T(8,128)S(1)} %dynamic-slice_bitcast_fusion), channel_id=1, source_target_pairs={{0,32},{32,0},{64,96},{96,64},{128,160},{160,128},{192,224},{224,1... | collective-permute-start | bytes 786440 | tf_op jit(solution)/shard_map/ppermute | solution.py:33
  147.5 6.6 %collective-permute-start.1 = (f32[4,16,512]{2,1,0:T(8,128)S(1)}, f32[4,16,512]{2,1,0:T(8,128)S(1)}, u32[]{:S(2)}, u32[]{:S(2)}) collective-permute-start(f32[4,16,512]{2,1,0:T(8,128)S(1)} %dynamic-slice_bitcast_fusion.1), channel_id=1, source_target_pairs={{0,64},{32,96},{64,0},{96,32},{128,192},{160,224},{192,128},{224,1... | collective-permute-start | bytes 393224 | tf_op jit(solution)/shard_map/ppermute | solution.py:33
  154.1 11.4 %collective-permute-start.2 = (f32[1,16,512]{2,1,0:T(8,128)S(1)}, f32[1,16,512]{2,1,0:T(8,128)S(1)}, u32[]{:S(2)}, u32[]{:S(2)}) collective-permute-start(f32[1,16,512]{2,1,0:T(8,128)S(1)} %get-tuple-element.6), channel_id=1, source_target_pairs={{0,128},{32,160},{64,192},{96,224},{128,0},{160,32},{192,64},{224,... | collective-permute-start | bytes 98312 | tf_op jit(solution)/shard_map/ppermute | solution.py:33
  156.3 9.2 %collective-permute-start.3 = (f32[1,16,512]{2,1,0:T(8,128)S(1)}, f32[1,16,512]{2,1,0:T(8,128)S(1)}, u32[]{:S(2)}, u32[]{:S(2)}) collective-permute-start(f32[1,16,512]{2,1,0:T(8,128)S(1)} %get-tuple-element.8), channel_id=1, source_target_pairs={{0,256},{32,288},{64,320},{96,352},{128,384},{160,416},{192,448},{... | collective-permute-start | bytes 98312 | tf_op jit(solution)/shard_map/ppermute | solution.py:33
  160.3 7.5 %collective-permute-start.4 = (f32[1,16,512]{2,1,0:T(8,128)S(1)}, f32[1,16,512]{2,1,0:T(8,128)S(1)}, u32[]{:S(2)}, u32[]{:S(2)}) collective-permute-start(f32[1,16,512]{2,1,0:T(8,128)S(1)} %get-tuple-element.7), channel_id=1, source_target_pairs={{0,384},{32,416},{64,448},{96,480},{128,256},{160,288},{192,320},{... | collective-permute-start | bytes 98312 | tf_op jit(solution)/shard_map/ppermute | solution.py:33

commit v6 on v5

--- a/solution.py
+++ b/solution.py
@@ -8,11 +8,13 @@
 
 ITERS = 3
 LANES = 128
+Y_CHIPS = 8
 
 
-def spread(block, axis):
-    n = lax.axis_size(axis)
-    return lax.all_to_all(jnp.broadcast_to(block[None], (n,) + block.shape), axis, 0, 0)
+def spread(block, axis, groups=None):
+    n = lax.axis_size(axis) if groups is None else len(groups[0])
+    copies = jnp.broadcast_to(block[None], (n,) + block.shape)
+    return lax.all_to_all(copies, axis, 0, 0, axis_index_groups=groups)
 
 
 def swap(chunks, axis):
@@ -48,7 +50,11 @@
 
 
 def gather_parts(graph_part, conf_part):
-    graph_t = spread(graph_part, "col")
+    x_chips = lax.axis_size("col") // Y_CHIPS
+    same_x = [[x * Y_CHIPS + y for y in range(Y_CHIPS)] for x in range(x_chips)]
+    same_y = [[x * Y_CHIPS + y for x in range(x_chips)] for y in range(Y_CHIPS)]
+    along_y = spread(graph_part, "col", same_x)
+    graph_t = spread(along_y, "col", same_y)
     conf_t = lax.all_gather(conf_part, "row")
     return graph_t.reshape(-1, graph_part.shape[1]), conf_t.reshape(-1, conf_part.shape[1])
 

time: 171 us -> 173 us (1.012)
  blocking collectives: 99.1 us -> 107 us
  starting transfers between devices: 35.9 us -> 30.3 us
    all_to_all x5 -> x6, blocking collectives: 73.7 us -> 79.7 us  [spread(): return lax.all_to_all(copies, axis, 0, 0, axis_index_groups=groups)]
    all_to_all x2, starting transfers between devices: 16 us -> 10.4 us  [spread(): return lax.all_to_all(copies, axis, 0, 0, axis_index_groups=groups)]
where the time goes in v6:
time: 173 us; the launch traced here: 171 us
  blocking collectives  107 us (62%)
  starting transfers between devices  30.3 us (18%)
  waiting for transfers between devices  15.4 us (9%)
  matrix products  8.73 us (5%)
  other arithmetic  6.25 us (4%)
  local copies, waits for them, and re-layouts  2.88 us (2%)
    all_to_all x6, blocking collectives, spread(): return lax.all_to_all(copies, axis, 0, 0, axis_index_groups=groups)  79.7 us
    all_gather x1, blocking collectives, gather_parts(): conf_t = lax.all_gather(conf_part, 'row')  27 us
    ppermute x5, starting transfers between devices, fold(): chunks = chunks + lax.ppermute(sent, axis, partner)  15.8 us
    all_to_all x2, starting transfers between devices, spread(): return lax.all_to_all(copies, axis, 0, 0, axis_index_groups=groups)  10.4 us
    dot_general x3, matrix products, matmul(): lax.dot_general(lhs, rhs, (contract, ((), ())), precision=precision, pref...  8.73 us
    ppermute x5, waiting for transfers between devices, fold(): chunks = chunks + lax.ppermute(sent, axis, partner)  7.89 us
    all_to_all x2, waiting for transfers between devices, spread(): return lax.all_to_all(copies, axis, 0, 0, axis_index_groups=groups)  7.48 us
    all_to_all x1, starting transfers between devices, swap(): return lax.all_to_all(chunks, axis, 0, 0)  4.11 us
  transfers between devices with their start and end apart: 8, of which 4 were waited for; matrix products, arithmetic and copies ran while one was open for 3% of the time, Pallas kernels for 0%

profile of v6, /device:TPU:1, one launch (start us, length us, event | category | flops | bytes accessed | tf_op | source)
XLA Modules:
  0.0 171.1 jit_solution(18172645077788550743)
XLA Ops:
  0.6 0.8 broadcast_in_dim.16
  1.4 17.0 %all_to_all.45 = f32[8,8,1024]{2,1,0:T(8,128)S(1)} all-to-all(f32[8,8,1024]{2,1,0:T(8,128)S(1)} %broadcast_in_dim.16), channel_id=1, replica_groups={{0,1,2,3,4,5,6,7},{8,9,10,11,12,13,14,15},{16,17,18,19,20,21,22,23},{24..., dimensions={0} | all-to-all | bytes 524288 | tf_op jit(solution)/shard_map/all_to_all | solution.py:17
  18.4 1.2 broadcast_in_dim.17
  19.6 5.0 %all-to-all-start.1 = ((f32[4,8,8,1024]{3,2,1,0:T(8,128)}), f32[4,8,8,1024]{3,2,1,0:T(8,128)}, u32[]{:S(2)}, u32[]{:S(2)}) async-start(f32[4,8,8,1024]{3,2,1,0:T(8,128)} %broadcast_in_dim.17), calls=%async_computation.1 | async-start | bytes 2097152 | tf_op jit(solution)/shard_map/all_to_all | solution.py:17
  24.5 27.0 %all-gather = f32[256,512]{1,0:T(8,128)S(1)} all-gather(f32[16,512]{1,0:T(8,128)S(1)} %bitcast.58), channel_id=2, replica_groups=mesh['row'=16,'col'=32] {'row'}, dimensions={0}, use_global_device_ids=true | all-gather | bytes 557056 | tf_op jit(solution)/shard_map/all_gather | solution.py:58
  51.6 3.2 %fusion.17 = (f32[1024]{0:T(1024)S(1)}, f32[1024,512]{1,0:T(8,128)S(1)}) fusion(f32[256,1024]{1,0:T(8,128)} %bitcast.1, f32[256,512]{1,0:T(8,128)S(1)} %all-gather), kind=kOutput, calls=%fused_computation.53 | convolution fusion | flops 1611660288 | bytes 3674112 | tf_op jit(solution)/shard_map/dot_general | solution.py:63
  54.7 0.7 exponential_reduce_fusion.4
  55.5 13.9 %all_to_all.46 = f32[32,8,128]{2,1,0:T(8,128)S(1)} all-to-all(f32[32,8,128]{2,1,0:T(8,128)S(1)} %broadcast_in_dim.18), channel_id=1, replica_groups=mesh['row'=16,'col'=32] {'col'}, dimensions={0} | all-to-all | bytes 262144 | tf_op jit(solution)/shard_map/all_to_all | solution.py:17
  69.7 0.4 exponential_reduce_fusion.3
  70.1 12.0 %all_to_all.47 = f32[16,4,128]{2,1,0:T(4,128)S(1)} all-to-all(f32[16,4,128]{2,1,0:T(4,128)S(1)} %broadcast_in_dim.19), channel_id=1, replica_groups=mesh['row'=16,'col'=32] {'row'}, dimensions={0} | all-to-all | bytes 65536 | tf_op jit(solution)/shard_map/all_to_all | solution.py:17
  82.4 0.6 exponential_reduce_fusion.2
  83.0 12.4 %all_to_all.48 = f32[32,8,128]{2,1,0:T(8,128)S(1)} all-to-all(f32[32,8,128]{2,1,0:T(8,128)S(1)} %broadcast_in_dim.20), channel_id=1, replica_groups=mesh['row'=16,'col'=32] {'col'}, dimensions={0} | all-to-all | bytes 262144 | tf_op jit(solution)/shard_map/all_to_all | solution.py:17
  96.2 12.0 %all_to_all.49 = f32[16,4,128]{2,1,0:T(4,128)S(1)} all-to-all(f32[16,4,128]{2,1,0:T(4,128)S(1)} %broadcast_in_dim.21), channel_id=1, replica_groups=mesh['row'=16,'col'=32] {'row'}, dimensions={0} | all-to-all | bytes 65536 | tf_op jit(solution)/shard_map/all_to_all | solution.py:17
  108.5 0.6 exponential_reduce_fusion
  109.1 12.4 %all_to_all.50 = f32[32,8,128]{2,1,0:T(8,128)S(1)} all-to-all(f32[32,8,128]{2,1,0:T(8,128)S(1)} %broadcast_in_dim.22), channel_id=1, replica_groups=mesh['row'=16,'col'=32] {'col'}, dimensions={0} | all-to-all | bytes 262144 | tf_op jit(solution)/shard_map/all_to_all | solution.py:17
  121.8 0.4 fusion.5
  122.3 0.6 broadcast_in_dim.23
  122.9 5.4 %all-to-all-start.7 = ((f32[16,4,128]{2,1,0:T(4,128)}), f32[16,4,128]{2,1,0:T(4,128)S(1)}, u32[]{:S(2)}, u32[]{:S(2)}) async-start(f32[16,4,128]{2,1,0:T(4,128)} %broadcast_in_dim.23), calls=%async_computation.7 | async-start | bytes 65536 | tf_op jit(solution)/shard_map/all_to_all | solution.py:17
  128.3 7.5 %all-to-all-done.7 = f32[16,4,128]{2,1,0:T(4,128)S(1)} async-done(((f32[16,4,128]{2,1,0:T(4,128)}), f32[16,4,128]{2,1,0:T(4,128)S(1)}, u32[]{:S(2)}, u32[]{:S(2)}) %all-to-all-start.7) | async-done | bytes 32800 | tf_op jit(solution)/shard_map/all_to_all | solution.py:17
  135.9 2.3 %fusion.9 = f32[32,8,1024]{2,1,0:T(8,128)} fusion(f32[256,512]{1,0:T(8,128)S(1)} %all-gather, f32[1024,512]{1,0:T(8,128)S(1)} %get-tuple-element.10, f32[512]{0:T(512)S(1)} %get-tuple-element.5, f32[1024]{0:T(1024)S(1)} %subtract_bitcast_fusion), kind=kOutput, calls=%fused_computation.19 | convolution fusion | flops 806617088 | bytes 3676160 | tf_op jit(solution)/shard_map/dot_general | solution.py:63
  138.2 4.1 %all-to-all-start.8 = ((f32[32,8,1024]{2,1,0:T(8,128)}), f32[32,8,1024]{2,1,0:T(8,128)S(1)}, u32[]{:S(2)}, u32[]{:S(2)}) async-start(f32[32,8,1024]{2,1,0:T(8,128)} %fusion.9), calls=%async_computation.8 | async-start | bytes 2097152 | tf_op jit(solution)/shard_map/all_to_all | solution.py:21
  142.3 3.2 %fusion.12 = f32[256,512]{0,1:T(8,128)S(1)} fusion(f32[256,1024]{1,0:T(8,128)} %bitcast.1, f32[1024,512]{1,0:T(8,128)S(1)} %get-tuple-element.10, f32[512]{0:T(512)S(1)} %add_reduce_fusion, f32[1024]{0:T(1024)S(1)} %subtract_bitcast_fusion), kind=kOutput, calls=%fused_computation.20 | convolution fusion | flops 806354944 | bytes 3676160 | tf_op jit(solution)/shard_map/dot_general | solution.py:63
  145.9 2.3 %collective-permute-start = (f32[8,16,512]{2,1,0:T(8,128)S(1)}, f32[8,16,512]{2,1,0:T(8,128)S(1)}, u32[]{:S(2)}, u32[]{:S(2)}) collective-permute-start(f32[8,16,512]{2,1,0:T(8,128)S(1)} %dynamic-slice_bitcast_fusion), channel_id=1, source_target_pairs={{0,32},{32,0},{64,96},{96,64},{128,160},{160,128},{192,224},{224,1... | collective-permute-start | bytes 786440 | tf_op jit(solution)/shard_map/ppermute | solution.py:35
  148.3 1.1 collective-permute-done
  149.5 2.1 %collective-permute-start.1 = (f32[4,16,512]{2,1,0:T(8,128)S(1)}, f32[4,16,512]{2,1,0:T(8,128)S(1)}, u32[]{:S(2)}, u32[]{:S(2)}) collective-permute-start(f32[4,16,512]{2,1,0:T(8,128)S(1)} %dynamic-slice_bitcast_fusion.1), channel_id=1, source_target_pairs={{0,64},{32,96},{64,0},{96,32},{128,192},{160,224},{192,128},{224,1... | collective-permute-start | bytes 393224 | tf_op jit(solution)/shard_map/ppermute | solution.py:35
  151.6 4.4 %collective-permute-done.1 = f32[4,16,512]{2,1,0:T(8,128)S(1)} collective-permute-done((f32[4,16,512]{2,1,0:T(8,128)S(1)}, f32[4,16,512]{2,1,0:T(8,128)S(1)}, u32[]{:S(2)}, u32[]{:S(2)}) %collective-permute-start.1) | collective-permute-done | bytes 131104 | tf_op jit(solution)/shard_map/ppermute | solution.py:35
  156.1 2.2 %collective-permute-start.2 = (f32[1,16,512]{2,1,0:T(8,128)S(1)}, f32[1,16,512]{2,1,0:T(8,128)S(1)}, u32[]{:S(2)}, u32[]{:S(2)}) collective-permute-start(f32[1,16,512]{2,1,0:T(8,128)S(1)} %get-tuple-element.6), channel_id=1, source_target_pairs={{0,128},{32,160},{64,192},{96,224},{128,0},{160,32},{192,64},{224,... | collective-permute-start | bytes 98312 | tf_op jit(solution)/shard_map/ppermute | solution.py:35
  158.3 3.9 %collective-permute-start.3 = (f32[1,16,512]{2,1,0:T(8,128)S(1)}, f32[1,16,512]{2,1,0:T(8,128)S(1)}, u32[]{:S(2)}, u32[]{:S(2)}) collective-permute-start(f32[1,16,512]{2,1,0:T(8,128)S(1)} %get-tuple-element.8), channel_id=1, source_target_pairs={{0,256},{32,288},{64,320},{96,352},{128,384},{160,416},{192,448},{... | collective-permute-start | bytes 98312 | tf_op jit(solution)/shard_map/ppermute | solution.py:35
  162.3 5.2 %collective-permute-start.4 = (f32[1,16,512]{2,1,0:T(8,128)S(1)}, f32[1,16,512]{2,1,0:T(8,128)S(1)}, u32[]{:S(2)}, u32[]{:S(2)}) collective-permute-start(f32[1,16,512]{2,1,0:T(8,128)S(1)} %get-tuple-element.7), channel_id=1, source_target_pairs={{0,384},{32,416},{64,448},{96,480},{128,256},{160,288},{192,320},{... | collective-permute-start | bytes 98312 | tf_op jit(solution)/shard_map/ppermute | solution.py:35
  167.5 2.3 %collective-permute-done.4 = f32[1,16,512]{2,1,0:T(8,128)S(1)} collective-permute-done((f32[1,16,512]{2,1,0:T(8,128)S(1)}, f32[1,16,512]{2,1,0:T(8,128)S(1)}, u32[]{:S(2)}, u32[]{:S(2)}) %collective-permute-start.4) | collective-permute-done | bytes 32800 | tf_op jit(solution)/shard_map/ppermute | solution.py:35
  169.8 0.6 add_bitcast_fusion
  170.4 0.7 reduce_sum.129
  (52 shorter events, 2.6 us)
Async XLA Ops:
  0.6 23.9 %copy-start.1 = (f32[512,16]{0,1:T(8,128)S(1)}, f32[512,16]{0,1:T(8,128)}, u32[]{:S(2)}) copy-start(f32[512,16]{0,1:T(8,128)} %param.3) | copy-start | bytes 98308
  19.6 32.0 %all-to-all-start.1 = ((f32[4,8,8,1024]{3,2,1,0:T(8,128)}), f32[4,8,8,1024]{3,2,1,0:T(8,128)}, u32[]{:S(2)}, u32[]{:S(2)}) async-start(f32[4,8,8,1024]{3,2,1,0:T(8,128)} %broadcast_in_dim.17), calls=%async_computation.1 | async-start | bytes 2097152 | tf_op jit(solution)/shard_map/all_to_all | solution.py:17
  121.6 20.7 %copy-start = (f32[1024]{0:T(1024)}, f32[1024]{0:T(1024)S(1)}, u32[]{:S(2)}) copy-start(f32[1024]{0:T(1024)S(1)} %subtract_bitcast_fusion) | copy-start | bytes 12292
  122.9 12.9 %all-to-all-start.7 = ((f32[16,4,128]{2,1,0:T(4,128)}), f32[16,4,128]{2,1,0:T(4,128)S(1)}, u32[]{:S(2)}, u32[]{:S(2)}) async-start(f32[16,4,128]{2,1,0:T(4,128)} %broadcast_in_dim.23), calls=%async_computation.7 | async-start | bytes 65536 | tf_op jit(solution)/shard_map/all_to_all | solution.py:17
  135.9 2.3 %copy-start.2 = (f32[512]{0:T(512)}, f32[512]{0:T(512)S(1)}, u32[]{:S(2)}) copy-start(f32[512]{0:T(512)S(1)} %get-tuple-element.5) | copy-start | bytes 6148
  138.2 32.2 %all-to-all-start.8 = ((f32[32,8,1024]{2,1,0:T(8,128)}), f32[32,8,1024]{2,1,0:T(8,128)S(1)}, u32[]{:S(2)}, u32[]{:S(2)}) async-start(f32[32,8,1024]{2,1,0:T(8,128)} %fusion.9), calls=%async_computation.8 | async-start | bytes 2097152 | tf_op jit(solution)/shard_map/all_to_all | solution.py:21
  145.9 3.5 %collective-permute-start = (f32[8,16,512]{2,1,0:T(8,128)S(1)}, f32[8,16,512]{2,1,0:T(8,128)S(1)}, u32[]{:S(2)}, u32[]{:S(2)}) collective-permute-start(f32[8,16,512]{2,1,0:T(8,128)S(1)} %dynamic-slice_bitcast_fusion), channel_id=1, source_target_pairs={{0,32},{32,0},{64,96},{96,64},{128,160},{160,128},{192,224},{224,1... | collective-permute-start | bytes 786440 | tf_op jit(solution)/shard_map/ppermute | solution.py:35
  149.5 6.6 %collective-permute-start.1 = (f32[4,16,512]{2,1,0:T(8,128)S(1)}, f32[4,16,512]{2,1,0:T(8,128)S(1)}, u32[]{:S(2)}, u32[]{:S(2)}) collective-permute-start(f32[4,16,512]{2,1,0:T(8,128)S(1)} %dynamic-slice_bitcast_fusion.1), channel_id=1, source_target_pairs={{0,64},{32,96},{64,0},{96,32},{128,192},{160,224},{192,128},{224,1... | collective-permute-start | bytes 393224 | tf_op jit(solution)/shard_map/ppermute | solution.py:35
  156.1 11.4 %collective-permute-start.2 = (f32[1,16,512]{2,1,0:T(8,128)S(1)}, f32[1,16,512]{2,1,0:T(8,128)S(1)}, u32[]{:S(2)}, u32[]{:S(2)}) collective-permute-start(f32[1,16,512]{2,1,0:T(8,128)S(1)} %get-tuple-element.6), channel_id=1, source_target_pairs={{0,128},{32,160},{64,192},{96,224},{128,0},{160,32},{192,64},{224,... | collective-permute-start | bytes 98312 | tf_op jit(solution)/shard_map/ppermute | solution.py:35
  158.3 9.2 %collective-permute-start.3 = (f32[1,16,512]{2,1,0:T(8,128)S(1)}, f32[1,16,512]{2,1,0:T(8,128)S(1)}, u32[]{:S(2)}, u32[]{:S(2)}) collective-permute-start(f32[1,16,512]{2,1,0:T(8,128)S(1)} %get-tuple-element.8), channel_id=1, source_target_pairs={{0,256},{32,288},{64,320},{96,352},{128,384},{160,416},{192,448},{... | collective-permute-start | bytes 98312 | tf_op jit(solution)/shard_map/ppermute | solution.py:35
  162.3 7.6 %collective-permute-start.4 = (f32[1,16,512]{2,1,0:T(8,128)S(1)}, f32[1,16,512]{2,1,0:T(8,128)S(1)}, u32[]{:S(2)}, u32[]{:S(2)}) collective-permute-start(f32[1,16,512]{2,1,0:T(8,128)S(1)} %get-tuple-element.7), channel_id=1, source_target_pairs={{0,384},{32,416},{64,448},{96,480},{128,256},{160,288},{192,320},{... | collective-permute-start | bytes 98312 | tf_op jit(solution)/shard_map/ppermute | solution.py:35
